TPU v7x, 256 devices: a whole 4x4x8 slice. The times are simulated.
256 devices in a mesh: gx: 2 (over z_hi), gy: 64 (over z_lo, y, x), gz: 2 (over core).
Axes of the slice: x: 4, y: 4, z: 8 (z_hi: 2, z_lo: 4; z = z_hi * 4 + z_lo), core: 2. Of those that a mesh axis runs over, the one named last changes fastest.
Arguments:
- estimate: float32 [256, 64, 4096], P(('gx', 'gy', 'gz')), may hold values from 0.5 to 4
- views_data: bfloat16 [4, 256, 64, 4096], P(None, ('gx', 'gy', 'gz')), may hold values from 0.099609375 to 10
- point_spread: float32 [4, 2, 3, 23], replicated, as said below
- block_owner: int32 [2, 64, 4], replicated, may hold values from -1 to 1, as said below
Outputs:
- updated: float32 [256, 64, 4096], P(('gx', 'gy', 'gz'))
Inputs may be any that keep to these rules, and one draw needn't show every extreme that they name: `block_owner`: entry g + s names slot s of the device at position g along gz in the same column (the first two indices are the positions along gx and gy); -1 marks background. Each code appears at most once in a column, the named blocks of a column are consecutive along the third index, and in some column every code from 0 to 1 × (size of gz) − 1 appears. Slots that no entry names are empty and their rows of estimate and views_data are not used. `point_spread`: taps of term 0 are positive.
All inputs are finite; a program needn't handle non-finite values.
Results may differ from a plain program's by a relative error of at most 0.00095.
Values may be sent and summed in bfloat16 or wider, within the bound.
A program may use at most 128 MiB of HBM per device.

v0:
```python
import functools

import jax
import jax.numpy as jnp
from jax import lax
from jax.experimental import pallas as pl
from jax.experimental.pallas import tpu as pltpu
from jax.sharding import PartitionSpec as P

MESH = pl.DeviceIdType.MESH
F32, BF16, I32 = jnp.float32, jnp.bfloat16, jnp.int32
BLOCK, TAPS, HALO, RANK, VIEWS, PILLAR = 64, 23, 11, 2, 4, 4
FLOOR = 0.5
SPAN_A = 80
PAIRS = 48
STEP_F, STEP_T, STEP_V = 56, 168, 520
LANES = 128
WIDTH = 768
FACE = 3328


def iota(shape, dim):
    return lax.broadcasted_iota(I32, shape, dim)


def band(distance, tap):
    total = jnp.zeros(distance.shape, F32)
    for t in range(TAPS):
        total = jnp.where(distance == t, tap(t), total)
    return total


def ext_c(lane):
    return jnp.where(lane < 96, lane, lane - LANES)


def parity_b(row):
    return jnp.where(row < 32, 2 * row, 2 * row - 63)


def ext_b(row):
    odd = (row >= PAIRS).astype(I32)
    pair = row - PAIRS * odd
    value = 2 * pair + odd - 88 * (pair >= 38).astype(I32)
    return jnp.where(pair >= 44, 1000, value)


def build_weights(ps, mesh_row, wb, wbt, wc, wct, wa, wat):
    def tap(number, axis):
        return lambda t: ps[(number * 3 + axis) * TAPS + t]

    d_b = ext_b(iota((64, 96), 1)) - parity_b(iota((64, 96), 0)) + HALO
    lane = iota((LANES, LANES), 1)
    d_c = ext_c(iota((LANES, LANES), 0)) - jnp.where(lane >= 64, lane - 64, lane) + HALO
    d_ct = ext_c(iota((64, LANES), 1)) - iota((64, LANES), 0) + HALO
    wct[...] = jnp.zeros_like(wct)

    @pl.loop(0, VIEWS * RANK)
    def _(number):
        start = pl.multiple_of(number * 64, 64)
        wb[pl.ds(start, 64), :] = band(d_b, tap(number, 1)).astype(BF16)
        base = band(d_c, tap(number, 2))
        wc[number, 0:128, :] = jnp.where(lane < 64, base, 0.0).astype(BF16)
        wc[number, 128:256, :] = jnp.where(lane >= 64, base, 0.0).astype(BF16)
        base = band(d_ct, tap(number, 2)).astype(BF16)
        wct[number, 0:64, 0:128] = base
        wct[number, 64:128, 128:256] = base

    col = iota((96, LANES), 1)
    high = col >= 64
    d_bt = ext_b(iota((96, LANES), 0)) - parity_b(jnp.where(high, col - 64, col)) + HALO
    for pair in range(VIEWS * RANK // 2):
        low_tap, high_tap = tap(2 * pair, 1), tap(2 * pair + 1, 1)
        wbt[:, pair * LANES : (pair + 1) * LANES] = band(
            d_bt, lambda t: jnp.where(high, high_tap(t), low_tap(t))
        ).astype(BF16)

    def ext_a(place):
        return place - SPAN_A * (place >= 64).astype(I32) * mesh_row

    second = iota((64, 2 * SPAN_A), 1) >= SPAN_A
    place = iota((64, 2 * SPAN_A), 1) - SPAN_A * second.astype(I32)
    d_a = ext_a(place) - iota((64, 2 * SPAN_A), 0) + HALO
    d_at = ext_a(iota((SPAN_A, 64), 0)) - iota((SPAN_A, 64), 1) + HALO

    @pl.loop(0, VIEWS)
    def _(view):
        first_tap, second_tap = tap(2 * view, 0), tap(2 * view + 1, 0)
        wa[view] = band(d_a, lambda t: jnp.where(second, second_tap(t), first_tap(t))).astype(BF16)
        wat[view, 0:SPAN_A, :] = band(d_at, first_tap).astype(BF16)
        wat[view, SPAN_A : 2 * SPAN_A, :] = band(d_at, second_tap).astype(BF16)


def kernel(
    n_gy,
    est_hbm,
    data_hbm,
    ps,
    owner,
    out,
    est,
    data,
    own,
    sib,
    gx_in,
    gy_in,
    co_in,
    mid_f,
    mix_f,
    rows_t,
    t2,
    v2,
    wb,
    wbt,
    wc,
    wct,
    wa,
    wat,
    keep_gx,
    keep_gy,
    keep_co,
    give_own,
    give_gx,
    give_gy,
    give_co,
    take_own,
    take_gx,
    take_gy,
    take_co,
    put_gx,
    put_gy,
    put_co,
    get_gx,
    get_gy,
    get_co,
    load_sem,
    send_sem,
    recv_sem,
):
    i, j, g = lax.axis_index("gx"), lax.axis_index("gy"), lax.axis_index("gz")
    sibling = (i, j, 1 - g)
    across = (1 - i, j, g)
    beside = ((i, j - 1, g), (i, j + 1, g))
    corner = ((1 - i, j - 1, g), (1 - i, j + 1, g))
    exists = (j > 0, j < n_gy - 1)

    load_est = pltpu.make_async_copy(est_hbm.at[0], est, load_sem.at[0])
    load_data = pltpu.make_async_copy(data_hbm.at[:, 0], data, load_sem.at[1])
    load_est.start()
    load_data.start()

    def copy(number, src, dst, target):
        return pltpu.make_async_remote_copy(
            src_ref=src,
            dst_ref=dst,
            send_sem=send_sem.at[number],
            recv_sem=recv_sem.at[number],
            device_id=target,
            device_id_type=MESH,
        )

    def both_sides(action):
        for side in range(2):

            @pl.when(exists[side])
            def _(side=side):
                action(side)

    barrier = pltpu.get_barrier_semaphore()
    for target in (sibling, across):
        pl.semaphore_signal(barrier, inc=1, device_id=target, device_id_type=MESH)

    def greet(side):
        pl.semaphore_signal(barrier, inc=1, device_id=beside[side], device_id_type=MESH)
        pl.semaphore_signal(barrier, inc=1, device_id=corner[side], device_id_type=MESH)

    both_sides(greet)
    load_est.wait()
    own[...] = est[...].astype(BF16)
    waits = 2 + 2 * exists[0].astype(I32) + 2 * exists[1].astype(I32)
    pl.semaphore_wait(barrier, waits)

    edge = pl.multiple_of(48 * (1 - i), 16)
    my_edge = own.at[pl.ds(edge, 16), :]
    toward = (pl.ds(0, WIDTH), pl.ds(FACE, WIDTH))
    send_sib = copy(0, own, sib, sibling)
    send_gx = copy(1, my_edge, gx_in.at[0], across)
    send_gy = [copy(2 + s, own.at[:, toward[s]], gy_in.at[1 - s, 0], beside[s]) for s in range(2)]
    send_co = [
        copy(4 + s, own.at[pl.ds(edge, 16), toward[s]], co_in.at[1 - s, 0], corner[s])
        for s in range(2)
    ]
    pass_gx = copy(6, gx_in.at[0], gx_in.at[1], sibling)
    pass_gy = [copy(7 + s, gy_in.at[s, 0], gy_in.at[s, 1], sibling) for s in range(2)]
    pass_co = [copy(9 + s, co_in.at[s, 0], co_in.at[s, 1], sibling) for s in range(2)]

    def arrived(number, dst):
        copy(number, dst, dst, sibling).wait_recv()

    send_gx.start()
    both_sides(lambda s: send_co[s].start())
    both_sides(lambda s: send_gy[s].start())
    send_sib.start()

    for side in range(2):

        @pl.when(jnp.logical_not(exists[side]))
        def _(side=side):
            gy_in[side] = jnp.zeros(gy_in.shape[1:], BF16)
            co_in[side] = jnp.zeros(co_in.shape[1:], BF16)

    def column(row, col):
        col = jnp.minimum(jnp.maximum(col, 0), n_gy - 1)
        base = (row * n_gy + col) * PILLAR
        codes = [owner[base + k] for k in range(PILLAR)]
        found = []
        for code in (g, 1 - g):
            hits = [(codes[k] == code).astype(I32) for k in range(PILLAR)]
            found.append((sum(hits), sum(k * hits[k] for k in range(PILLAR))))
        return found

    home = column(i, j)
    valid, height = home[0]

    def factors(entry, there=None):
        present, level = entry
        live = present * valid
        if there is not None:
            live = live * there.astype(I32)
        at = [(live * (level - height == d).astype(I32)).astype(F32) for d in (0, 1, -1)]
        lane_low = (iota((1, LANES), 1) & 63) < 32
        return at[0], jnp.where(lane_low, at[1], at[2])

    f_sib = factors(home[1])
    f_gx = [factors(e) for e in column(1 - i, j)]
    f_gy = [[factors(e, exists[s]) for e in column(i, j + 2 * s - 1)] for s in range(2)]
    f_co = [[factors(e, exists[s]) for e in column(1 - i, j + 2 * s - 1)] for s in range(2)]
    live = valid.astype(F32)

    build_weights(ps, i, wb, wbt, wc, wct, wa, wat)

    def place(first_row, count, pair, mid, mix):
        mid_f[pl.ds(first_row * STEP_F + pair, count, stride=STEP_F), :] = mid
        mix_f[pl.ds(first_row * STEP_F + pair, count, stride=STEP_F), :] = mix

    def tile(number):
        return pl.ds(pl.multiple_of(number * LANES, LANES), LANES)

    def blend(pieces, factor):
        first, second = pieces[0].astype(F32), pieces[1].astype(F32)
        return (
            first * factor[0][0] + second * factor[1][0],
            first * factor[0][1] + second * factor[1][1],
        )

    for pair in range(44, PAIRS):
        place(0, SPAN_A, pair, jnp.zeros((SPAN_A, LANES), F32), jnp.zeros((SPAN_A, LANES), F32))

    first_pair = (38, 32)

    for side in range(2):

        @pl.when(exists[side])
        def _(side=side):
            arrived(3 - side, gy_in.at[side, 0])
            pass_gy[side].start()

    send_sib.wait_recv()

    @pl.loop(0, 32)
    def _(pair):
        place(0, 64, pair, own[:, tile(pair)].astype(F32), sib[:, tile(pair)].astype(F32) * f_sib[1])

    both_sides(lambda s: pass_gy[s].wait_recv())
    for side in range(2):
        for pair in range(6):
            lanes = pl.ds(pair * LANES, LANES)
            mid, mix = blend([gy_in[side, k, :, lanes] for k in range(2)], f_gy[side])
            place(0, 64, first_pair[side] + pair, mid, mix)

    low = iota((PAIRS, LANES), 1) < 64

    def forward_chunk(chunk):
        for two in range(4):
            parts = []
            for one in range(2):
                start = pl.multiple_of((chunk * 8 + two * 2 + one) * STEP_F, 8)
                mid, mix = mid_f[pl.ds(start, PAIRS), :], mix_f[pl.ds(start, PAIRS), :]
                even = jnp.where(low, mid, pltpu.roll(mix, 64, 1))
                odd = jnp.where(low, pltpu.roll(mid, 64, 1), mix)
                parts.append(jnp.concatenate([even, odd], axis=0).astype(BF16))
            first = jnp.dot(wb[...], jnp.concatenate(parts, axis=1), preferred_element_type=F32)
            rows_t[:, two * 256 : two * 256 + 256] = first.astype(BF16)
        for number in range(VIEWS * RANK):
            view, term = number // RANK, number % RANK
            block = jnp.concatenate(
                [
                    jnp.concatenate(
                        [
                            rows_t[number * 64 : number * 64 + 32, a * LANES : (a + 1) * LANES],
                            rows_t[number * 64 + 32 : number * 64 + 64, a * LANES : (a + 1) * LANES],
                        ],
                        axis=1,
                    )
                    for a in range(8)
                ],
                axis=0,
            )
            second = jnp.dot(block, wc[number], preferred_element_type=F32)
            for a in range(8):
                start = view * 32 * STEP_T + term * SPAN_A + chunk * 8 + a
                t2[pl.ds(start, 32, stride=STEP_T), :] = second[a * 32 : a * 32 + 32, :]

    pl.loop(0, 8)(forward_chunk)

    arrived(1, gx_in.at[0])
    pass_gx.start()
    for side in range(2):

        @pl.when(exists[side])
        def _(side=side):
            arrived(5 - side, co_in.at[side, 0])
            pass_co[side].start()

    pass_gx.wait_recv()
    both_sides(lambda s: pass_co[s].wait_recv())

    @pl.loop(0, 32)
    def _(pair):
        mid, mix = blend([gx_in[k, :, tile(pair)] for k in range(2)], f_gx)
        place(64, 16, pair, mid, mix)

    for side in range(2):
        for pair in range(6):
            lanes = pl.ds(pair * LANES, LANES)
            mid, mix = blend([co_in[side, k, :, lanes] for k in range(2)], f_co[side])
            place(64, 16, first_pair[side] + pair, mid, mix)

    pl.loop(8, 10)(forward_chunk)
    load_data.wait()

    def turn(step):
        view, two = step // 16, step % 16
        start = pl.multiple_of((view * 32 + two * 2) * STEP_T, 8)
        fields = jnp.concatenate(
            [t2[pl.ds(start + k * STEP_T, 2 * SPAN_A), :].astype(BF16) for k in range(2)], axis=1
        )
        blurred = jnp.dot(wa[view], fields, preferred_element_type=F32)
        observed = data[view, :, pl.ds(pl.multiple_of(two * 256, 256), 256)].astype(F32)
        ratio = (observed / jnp.maximum(blurred, FLOOR) * live).astype(BF16)
        back = jnp.dot(wat[view], ratio, preferred_element_type=F32).astype(BF16)
        for term in range(RANK):
            rows = back[term * SPAN_A : (term + 1) * SPAN_A]
            block = jnp.concatenate([rows[:, :LANES], rows[:, LANES:]], axis=0)
            wide = jnp.dot(block, wct[view * RANK + term], preferred_element_type=F32)
            for k in range(2):
                for odd in range(2):
                    at = (view * RANK + term) * 64 + odd * 32 + two * 2 + k
                    v2[pl.ds(at, SPAN_A, stride=STEP_V), :] = wide[
                        k * SPAN_A : (k + 1) * SPAN_A, odd * LANES : (odd + 1) * LANES
                    ]

    pl.loop(0, 64)(turn)

    def adjoint_pair(step):
        start = pl.multiple_of(step * 2 * STEP_V, 8)
        fields = jnp.concatenate(
            [v2[pl.ds(start + k * STEP_V, 512), :].astype(BF16) for k in range(2)], axis=1
        )
        spread = jnp.dot(wbt[...], fields, preferred_element_type=F32)
        for k in range(2):
            even = spread[0:PAIRS, k * LANES : (k + 1) * LANES]
            odd = spread[PAIRS : 2 * PAIRS, k * LANES : (k + 1) * LANES]
            at = pl.multiple_of((step * 2 + k) * STEP_F, 8)
            mid_f[pl.ds(at, PAIRS), :] = jnp.where(low, even, pltpu.roll(odd, 64, 1))
            mix_f[pl.ds(at, PAIRS), :] = jnp.where(low, pltpu.roll(even, 64, 1), odd)

    def fetch(first_row, count, pair):
        at = pl.ds(first_row * STEP_F + pair, count, stride=STEP_F)
        return mid_f[at, :], mix_f[at, :]

    pl.loop(32, 40)(adjoint_pair)

    @pl.loop(0, 32)
    def _(pair):
        mid, mix = fetch(64, 16, pair)
        keep_gx[:, tile(pair)] = mid * f_gx[0][0] + mix * f_gx[0][1]
        give_gx[:, tile(pair)] = (mid * f_gx[1][0] + mix * f_gx[1][1]).astype(BF16)

    for side in range(2):
        for pair in range(6):
            lanes = pl.ds(pair * LANES, LANES)
            mid, mix = fetch(64, 16, first_pair[side] + pair)
            one, two = f_co[side]
            keep_co[side, :, lanes] = mid * one[0] + mix * one[1]
            give_co[side, :, lanes] = (mid * two[0] + mix * two[1]).astype(BF16)

    share_gx = copy(11, give_gx, take_gx, sibling)
    share_co = copy(12, give_co, take_co, sibling)
    share_gx.start()
    share_co.start()
    pl.loop(0, 8)(adjoint_pair)
    share_gx.wait_recv()
    share_co.wait_recv()
    put_gx[...] = (keep_gx[...] + take_gx[...].astype(F32)).astype(BF16)
    put_co[...] = (keep_co[...] + take_co[...].astype(F32)).astype(BF16)
    final_gx = copy(13, put_gx, get_gx, across)
    final_co = [copy(14 + s, put_co.at[s], get_co.at[1 - s], corner[s]) for s in range(2)]
    final_gx.start()
    both_sides(lambda s: final_co[s].start())
    pl.loop(8, 32)(adjoint_pair)

    for side in range(2):
        for pair in range(6):
            lanes = pl.ds(pair * LANES, LANES)
            mid, mix = fetch(0, 64, first_pair[side] + pair)
            one, two = f_gy[side]
            keep_gy[side, :, lanes] = mid * one[0] + mix * one[1]
            give_gy[side, :, lanes] = (mid * two[0] + mix * two[1]).astype(BF16)

    share_gy = copy(16, give_gy, take_gy, sibling)
    share_gy.start()

    @pl.loop(0, 32)
    def _(pair):
        mid, mix = fetch(0, 64, pair)
        out[0, :, tile(pair)] = mid
        give_own[:, tile(pair)] = (mix * f_sib[1]).astype(BF16)

    share_own = copy(17, give_own, take_own, sibling)
    share_own.start()
    share_gy.wait_recv()
    put_gy[...] = (keep_gy[...] + take_gy[...].astype(F32)).astype(BF16)
    final_gy = [copy(18 + s, put_gy.at[s], get_gy.at[1 - s], beside[s]) for s in range(2)]
    both_sides(lambda s: final_gy[s].start())

    share_own.wait_recv()
    out[0] = out[0] + take_own[...].astype(F32)
    final_gx.wait_recv()
    out[0, pl.ds(edge, 16), :] = out[0, pl.ds(edge, 16), :] + get_gx[...].astype(F32)
    for side in range(2):

        @pl.when(exists[side])
        def _(side=side):
            arrived(15 - side, get_co.at[side])
            arrived(19 - side, get_gy.at[side])
            out[0, :, toward[side]] = out[0, :, toward[side]] + get_gy[side].astype(F32)
            out[0, pl.ds(edge, 16), toward[side]] = out[0, pl.ds(edge, 16), toward[side]] + get_co[
                side
            ].astype(F32)

    out[0] = est[...] * out[0] * (live / VIEWS)

    for item in (send_sib, send_gx, pass_gx, share_gx, share_co, final_gx, share_gy, share_own):
        item.wait_send()

    def drain(side):
        for group in (send_gy, send_co, pass_gy, pass_co, final_co, final_gy):
            group[side].wait_send()

    both_sides(drain)


def solution(mesh):
    n_gy = mesh.shape["gy"]

    def body(estimate, views_data, point_spread, block_owner):
        slab, side, small = (16, 4096), (2, 64, WIDTH), (2, 16, WIDTH)
        scratch = [
            ((64, 4096), F32),
            ((VIEWS, 64, 4096), BF16),
            ((64, 4096), BF16),
            ((64, 4096), BF16),
            ((2, 16, 4096), BF16),
            ((2, 2, 64, WIDTH), BF16),
            ((2, 2, 16, WIDTH), BF16),
            ((SPAN_A * STEP_F, LANES), F32),
            ((SPAN_A * STEP_F, LANES), F32),
            ((512, 1024), BF16),
            ((VIEWS * 32 * STEP_T, LANES), F32),
            ((SPAN_A * STEP_V, LANES), F32),
            ((512, 96), BF16),
            ((96, 512), BF16),
            ((8, 256, 128), BF16),
            ((8, 128, 256), BF16),
            ((VIEWS, 64, 2 * SPAN_A), BF16),
            ((VIEWS, 2 * SPAN_A, 64), BF16),
            (slab, F32),
            (side, F32),
            (small, F32),
            ((64, 4096), BF16),
            (slab, BF16),
            (side, BF16),
            (small, BF16),
            ((64, 4096), BF16),
            (slab, BF16),
            (side, BF16),
            (small, BF16),
            (slab, BF16),
            (side, BF16),
            (small, BF16),
            (slab, BF16),
            (side, BF16),
            (small, BF16),
        ]
        any_spec = pl.BlockSpec(memory_space=pl.ANY)
        smem = pl.BlockSpec(memory_space=pltpu.SMEM)
        return pl.pallas_call(
            functools.partial(kernel, n_gy),
            out_shape=jax.ShapeDtypeStruct((1, 64, 4096), F32),
            in_specs=[any_spec, any_spec, smem, smem],
            out_specs=pl.BlockSpec(memory_space=pltpu.VMEM),
            scratch_shapes=[pltpu.VMEM(shape, kind) for shape, kind in scratch]
            + [
                pltpu.SemaphoreType.DMA((2,)),
                pltpu.SemaphoreType.DMA((20,)),
                pltpu.SemaphoreType.DMA((20,)),
            ],
            compiler_params=pltpu.CompilerParams(
                collective_id=0, has_side_effects=True, vmem_limit_bytes=60 * 2**20
            ),
        )(estimate, views_data, point_spread.reshape(-1), block_owner.reshape(-1))

    placed = (P(("gx", "gy", "gz"), None, None), P(None, ("gx", "gy", "gz"), None, None), P(), P())
    return jax.shard_map(
        body,
        mesh=mesh,
        in_specs=placed,
        out_specs=P(("gx", "gy", "gz"), None, None),
        check_vma=False,
    )
```

profile of v0, /device:TPU:33, one launch (start us, length us, event | category | flops | bytes accessed | tf_op | source)
XLA Modules:
  0.0 90.2 jit_solution(15326410805825589780)
XLA Ops:
  0.0 0.7 copy.5
  0.7 0.7 reshape.6.ps
  1.4 0.8 copy.6
  2.2 0.7 reshape.7.owner
  2.9 85.1 %shard_map.46 = f32[1,64,4096]{2,1,0:T(8,128)} custom-call(f32[1,64,4096]{2,1,0:T(8,128)} %est_hbm.1, bf16[4,1,64,4096]{3,2,1,0:T(8,128)(2,1)} %data_hbm.1, f32[552]{0:T(1024)} %reshape.6.ps, s32[512]{0:T(512)} %reshape.7.owner), custom_call_target="tpu_custom_call" | custom-call | tf_op jit(solution)/shard_map/pallas_call | solution.py:508
  88.0 2.3 %copy.8 = f32[1,64,4096]{2,1,0:T(8,128)} copy(f32[1,64,4096]{2,1,0:T(8,128)} %shard_map.46) | data formatting | bytes 2097152
where the time goes:
time: 90.5 us; the launch traced here: 90.2 us
  Pallas kernels  85.1 us (94%)
  local copies, waits for them, and re-layouts  5.16 us (6%)
    pallas_call x1, Pallas kernels, body(): pl.pallas_call(functools.partial(kernel, n_gy), out_shape=jax.ShapeDtypeS...  85.1 us
    unnamed x3, local copies, waits for them, and re-layouts  3.76 us

commit v1 on v0

--- a/solution.py
+++ b/solution.py
@@ -17,6 +17,9 @@
 LANES = 128
 WIDTH = 768
 FACE = 3328
+TURN = 32
+CHUNK = 16
+DUO = 16
 
 
 def iota(shape, dim):
@@ -47,7 +50,7 @@
 
 def build_weights(ps, mesh_row, wb, wbt, wc, wct, wa, wat):
     def tap(number, axis):
-        return lambda t: ps[(number * 3 + axis) * TAPS + t]
+        return lambda t: ps[number // RANK, axis, number % RANK, t]
 
     d_b = ext_b(iota((64, 96), 1)) - parity_b(iota((64, 96), 0)) + HALO
     lane = iota((LANES, LANES), 1)
@@ -211,8 +214,7 @@
 
     def column(row, col):
         col = jnp.minimum(jnp.maximum(col, 0), n_gy - 1)
-        base = (row * n_gy + col) * PILLAR
-        codes = [owner[base + k] for k in range(PILLAR)]
+        codes = [owner[row, k, col] for k in range(PILLAR)]
         found = []
         for code in (g, 1 - g):
             hits = [(codes[k] == code).astype(I32) for k in range(PILLAR)]
@@ -281,10 +283,10 @@
     low = iota((PAIRS, LANES), 1) < 64
 
     def forward_chunk(chunk):
-        for two in range(4):
+        for two in range(CHUNK // 2):
             parts = []
             for one in range(2):
-                start = pl.multiple_of((chunk * 8 + two * 2 + one) * STEP_F, 8)
+                start = pl.multiple_of((chunk * CHUNK + two * 2 + one) * STEP_F, 8)
                 mid, mix = mid_f[pl.ds(start, PAIRS), :], mix_f[pl.ds(start, PAIRS), :]
                 even = jnp.where(low, mid, pltpu.roll(mix, 64, 1))
                 odd = jnp.where(low, pltpu.roll(mid, 64, 1), mix)
@@ -293,25 +295,26 @@
             rows_t[:, two * 256 : two * 256 + 256] = first.astype(BF16)
         for number in range(VIEWS * RANK):
             view, term = number // RANK, number % RANK
+            top = number * 64
             block = jnp.concatenate(
                 [
                     jnp.concatenate(
                         [
-                            rows_t[number * 64 : number * 64 + 32, a * LANES : (a + 1) * LANES],
-                            rows_t[number * 64 + 32 : number * 64 + 64, a * LANES : (a + 1) * LANES],
+                            rows_t[top : top + 32, a * LANES : (a + 1) * LANES],
+                            rows_t[top + 32 : top + 64, a * LANES : (a + 1) * LANES],
                         ],
                         axis=1,
                     )
-                    for a in range(8)
+                    for a in range(CHUNK)
                 ],
                 axis=0,
             )
             second = jnp.dot(block, wc[number], preferred_element_type=F32)
-            for a in range(8):
-                start = view * 32 * STEP_T + term * SPAN_A + chunk * 8 + a
+            for a in range(CHUNK):
+                start = view * 32 * STEP_T + term * SPAN_A + chunk * CHUNK + a
                 t2[pl.ds(start, 32, stride=STEP_T), :] = second[a * 32 : a * 32 + 32, :]
 
-    pl.loop(0, 8)(forward_chunk)
+    pl.loop(0, 64 // CHUNK)(forward_chunk)
 
     arrived(1, gx_in.at[0])
     pass_gx.start()
@@ -336,42 +339,44 @@
             mid, mix = blend([co_in[side, k, :, lanes] for k in range(2)], f_co[side])
             place(64, 16, first_pair[side] + pair, mid, mix)
 
-    pl.loop(8, 10)(forward_chunk)
+    pl.loop(64 // CHUNK, SPAN_A // CHUNK)(forward_chunk)
     load_data.wait()
 
     def turn(step):
-        view, two = step // 16, step % 16
-        start = pl.multiple_of((view * 32 + two * 2) * STEP_T, 8)
+        view, group = step // (32 // TURN), step % (32 // TURN)
+        start = pl.multiple_of((view * 32 + group * TURN) * STEP_T, 8)
         fields = jnp.concatenate(
-            [t2[pl.ds(start + k * STEP_T, 2 * SPAN_A), :].astype(BF16) for k in range(2)], axis=1
+            [t2[pl.ds(start + k * STEP_T, 2 * SPAN_A), :].astype(BF16) for k in range(TURN)], axis=1
         )
         blurred = jnp.dot(wa[view], fields, preferred_element_type=F32)
-        observed = data[view, :, pl.ds(pl.multiple_of(two * 256, 256), 256)].astype(F32)
-        ratio = (observed / jnp.maximum(blurred, FLOOR) * live).astype(BF16)
+        lanes = pl.ds(pl.multiple_of(group * (TURN * LANES), TURN * LANES), TURN * LANES)
+        ratio = (data[view, :, lanes].astype(F32) / jnp.maximum(blurred, FLOOR) * live).astype(BF16)
         back = jnp.dot(wat[view], ratio, preferred_element_type=F32).astype(BF16)
         for term in range(RANK):
             rows = back[term * SPAN_A : (term + 1) * SPAN_A]
-            block = jnp.concatenate([rows[:, :LANES], rows[:, LANES:]], axis=0)
+            block = jnp.concatenate(
+                [rows[:, k * LANES : (k + 1) * LANES] for k in range(TURN)], axis=0
+            )
             wide = jnp.dot(block, wct[view * RANK + term], preferred_element_type=F32)
-            for k in range(2):
+            for k in range(TURN):
                 for odd in range(2):
-                    at = (view * RANK + term) * 64 + odd * 32 + two * 2 + k
+                    at = (view * RANK + term) * 64 + odd * 32 + group * TURN + k
                     v2[pl.ds(at, SPAN_A, stride=STEP_V), :] = wide[
                         k * SPAN_A : (k + 1) * SPAN_A, odd * LANES : (odd + 1) * LANES
                     ]
 
-    pl.loop(0, 64)(turn)
-
-    def adjoint_pair(step):
-        start = pl.multiple_of(step * 2 * STEP_V, 8)
+    pl.loop(0, VIEWS * 32 // TURN)(turn)
+
+    def adjoint_rows(step):
+        start = pl.multiple_of(step * DUO * STEP_V, 8)
         fields = jnp.concatenate(
-            [v2[pl.ds(start + k * STEP_V, 512), :].astype(BF16) for k in range(2)], axis=1
+            [v2[pl.ds(start + k * STEP_V, 512), :].astype(BF16) for k in range(DUO)], axis=1
         )
         spread = jnp.dot(wbt[...], fields, preferred_element_type=F32)
-        for k in range(2):
+        for k in range(DUO):
             even = spread[0:PAIRS, k * LANES : (k + 1) * LANES]
             odd = spread[PAIRS : 2 * PAIRS, k * LANES : (k + 1) * LANES]
-            at = pl.multiple_of((step * 2 + k) * STEP_F, 8)
+            at = pl.multiple_of((step * DUO + k) * STEP_F, 8)
             mid_f[pl.ds(at, PAIRS), :] = jnp.where(low, even, pltpu.roll(odd, 64, 1))
             mix_f[pl.ds(at, PAIRS), :] = jnp.where(low, pltpu.roll(even, 64, 1), odd)
 
@@ -379,7 +384,7 @@
         at = pl.ds(first_row * STEP_F + pair, count, stride=STEP_F)
         return mid_f[at, :], mix_f[at, :]
 
-    pl.loop(32, 40)(adjoint_pair)
+    pl.loop(64 // DUO, SPAN_A // DUO)(adjoint_rows)
 
     @pl.loop(0, 32)
     def _(pair):
@@ -399,7 +404,7 @@
     share_co = copy(12, give_co, take_co, sibling)
     share_gx.start()
     share_co.start()
-    pl.loop(0, 8)(adjoint_pair)
+    pl.loop(0, 16 // DUO)(adjoint_rows)
     share_gx.wait_recv()
     share_co.wait_recv()
     put_gx[...] = (keep_gx[...] + take_gx[...].astype(F32)).astype(BF16)
@@ -408,7 +413,7 @@
     final_co = [copy(14 + s, put_co.at[s], get_co.at[1 - s], corner[s]) for s in range(2)]
     final_gx.start()
     both_sides(lambda s: final_co[s].start())
-    pl.loop(8, 32)(adjoint_pair)
+    pl.loop(16 // DUO, 64 // DUO)(adjoint_rows)
 
     for side in range(2):
         for pair in range(6):
@@ -476,7 +481,7 @@
             ((2, 2, 16, WIDTH), BF16),
             ((SPAN_A * STEP_F, LANES), F32),
             ((SPAN_A * STEP_F, LANES), F32),
-            ((512, 1024), BF16),
+            ((512, CHUNK * LANES), BF16),
             ((VIEWS * 32 * STEP_T, LANES), F32),
             ((SPAN_A * STEP_V, LANES), F32),
             ((512, 96), BF16),
@@ -519,7 +524,12 @@
             compiler_params=pltpu.CompilerParams(
                 collective_id=0, has_side_effects=True, vmem_limit_bytes=60 * 2**20
             ),
-        )(estimate, views_data, point_spread.reshape(-1), block_owner.reshape(-1))
+        )(
+            estimate,
+            views_data,
+            point_spread.transpose(0, 2, 1, 3),
+            block_owner.transpose(0, 2, 1),
+        )
 
     placed = (P(("gx", "gy", "gz"), None, None), P(None, ("gx", "gy", "gz"), None, None), P(), P())
     return jax.shard_map(

time: 90.5 us -> 60 us (0.66)
  Pallas kernels: 85.1 us -> 57.6 us
  local copies, waits for them, and re-layouts: 5.16 us -> 2.27 us
    pallas_call x1, Pallas kernels: 85.1 us -> 57.6 us  [body(): pl.pallas_call(functools.partial(kernel, n_gy), out_shape=jax.ShapeDtypeS...]
    unnamed x3 -> x1, local copies, waits for them, and re-layouts: 3.76 us -> 2.27 us
    reshape x2 -> x0, local copies, waits for them, and re-layouts: 1.39 us -> none  [the longest x1 0.7 us: body(): block_owner.reshape(-1)]
where the time goes in v1:
time: 60 us; the launch traced here: 59.8 us
  Pallas kernels  57.6 us (96%)
  local copies, waits for them, and re-layouts  2.27 us (4%)
    pallas_call x1, Pallas kernels, body(): pl.pallas_call(functools.partial(kernel, n_gy), out_shape=jax.ShapeDtypeS...  57.6 us
    unnamed x1, local copies, waits for them, and re-layouts  2.27 us

profile of v1, /device:TPU:33, one launch (start us, length us, event | category | flops | bytes accessed | tf_op | source)
XLA Modules:
  0.0 59.8 jit_solution(16754790677947478215)
XLA Ops:
  0.0 57.6 %shard_map.46 = f32[1,64,4096]{2,1,0:T(8,128)} custom-call(f32[1,64,4096]{2,1,0:T(8,128)} %est_hbm.1, bf16[4,1,64,4096]{3,2,1,0:T(8,128)(2,1)} %data_hbm.1, f32[4,3,2,23]{3,2,1,0:T(2,128)} %bitcast.2, s32[2,4,64]{2,1,0:T(4,128)} %bitcast.3), custom_call_target="tpu_custom_call" | custom-call | tf_op jit(solution)/shard_map/pallas_call | solution.py:513
  57.6 2.3 %copy.6 = f32[1,64,4096]{2,1,0:T(8,128)} copy(f32[1,64,4096]{2,1,0:T(8,128)} %shard_map.46) | data formatting | bytes 2097152

commit v2 on v1

--- a/solution.py
+++ b/solution.py
@@ -17,6 +17,7 @@
 LANES = 128
 WIDTH = 768
 FACE = 3328
+QUARTER = 1024
 TURN = 32
 CHUNK = 16
 DUO = 16
@@ -48,15 +49,18 @@
     return jnp.where(pair >= 44, 1000, value)
 
 
-def build_weights(ps, mesh_row, wb, wbt, wc, wct, wa, wat):
+def tap_of(ps):
     def tap(number, axis):
         return lambda t: ps[number // RANK, axis, number % RANK, t]
 
+    return tap
+
+
+def build_forward(ps, wb, wc):
+    tap = tap_of(ps)
     d_b = ext_b(iota((64, 96), 1)) - parity_b(iota((64, 96), 0)) + HALO
     lane = iota((LANES, LANES), 1)
     d_c = ext_c(iota((LANES, LANES), 0)) - jnp.where(lane >= 64, lane - 64, lane) + HALO
-    d_ct = ext_c(iota((64, LANES), 1)) - iota((64, LANES), 0) + HALO
-    wct[...] = jnp.zeros_like(wct)
 
     @pl.loop(0, VIEWS * RANK)
     def _(number):
@@ -65,6 +69,15 @@
         base = band(d_c, tap(number, 2))
         wc[number, 0:128, :] = jnp.where(lane < 64, base, 0.0).astype(BF16)
         wc[number, 128:256, :] = jnp.where(lane >= 64, base, 0.0).astype(BF16)
+
+
+def build_rest(ps, mesh_row, wbt, wct, wa, wat):
+    tap = tap_of(ps)
+    d_ct = ext_c(iota((64, LANES), 1)) - iota((64, LANES), 0) + HALO
+    wct[...] = jnp.zeros_like(wct)
+
+    @pl.loop(0, VIEWS * RANK)
+    def _(number):
         base = band(d_ct, tap(number, 2)).astype(BF16)
         wct[number, 0:64, 0:128] = base
         wct[number, 64:128, 128:256] = base
@@ -79,7 +92,8 @@
         ).astype(BF16)
 
     def ext_a(place):
-        return place - SPAN_A * (place >= 64).astype(I32) * mesh_row
+        inside = place - (64 + HALO) * (place >= 64).astype(I32) * mesh_row
+        return jnp.where(place >= 64 + HALO, 1000, inside)
 
     second = iota((64, 2 * SPAN_A), 1) >= SPAN_A
     place = iota((64, 2 * SPAN_A), 1) - SPAN_A * second.astype(I32)
@@ -105,6 +119,7 @@
     data,
     own,
     sib,
+    slab,
     gx_in,
     gy_in,
     co_in,
@@ -120,8 +135,8 @@
     wa,
     wat,
     keep_gx,
+    part_gx,
     keep_gy,
-    keep_co,
     give_own,
     give_gx,
     give_gy,
@@ -132,10 +147,8 @@
     take_co,
     put_gx,
     put_gy,
-    put_co,
     get_gx,
     get_gy,
-    get_co,
     load_sem,
     send_sem,
     recv_sem,
@@ -143,8 +156,7 @@
     i, j, g = lax.axis_index("gx"), lax.axis_index("gy"), lax.axis_index("gz")
     sibling = (i, j, 1 - g)
     across = (1 - i, j, g)
-    beside = ((i, j - 1, g), (i, j + 1, g))
-    corner = ((1 - i, j - 1, g), (1 - i, j + 1, g))
+    beside = [[(i, j + 2 * s - 1, g), (i, j + 2 * s - 1, 1 - g)] for s in range(2)]
     exists = (j > 0, j < n_gy - 1)
 
     load_est = pltpu.make_async_copy(est_hbm.at[0], est, load_sem.at[0])
@@ -174,35 +186,44 @@
         pl.semaphore_signal(barrier, inc=1, device_id=target, device_id_type=MESH)
 
     def greet(side):
-        pl.semaphore_signal(barrier, inc=1, device_id=beside[side], device_id_type=MESH)
-        pl.semaphore_signal(barrier, inc=1, device_id=corner[side], device_id_type=MESH)
+        for core in range(2):
+            pl.semaphore_signal(
+                barrier, inc=1, device_id=beside[side][core], device_id_type=MESH
+            )
 
     both_sides(greet)
     load_est.wait()
     own[...] = est[...].astype(BF16)
+
+    row = i.astype(F32)
+    edge = est[53:64, :] * (1.0 - row) + est[0:HALO, :] * row
+    slab[...] = jnp.concatenate(
+        [edge[:, q * QUARTER : (q + 1) * QUARTER] for q in range(4)] + [jnp.zeros((4, QUARTER), F32)],
+        axis=0,
+    ).astype(BF16)
     waits = 2 + 2 * exists[0].astype(I32) + 2 * exists[1].astype(I32)
     pl.semaphore_wait(barrier, waits)
 
-    edge = pl.multiple_of(48 * (1 - i), 16)
-    my_edge = own.at[pl.ds(edge, 16), :]
     toward = (pl.ds(0, WIDTH), pl.ds(FACE, WIDTH))
+    inside = ((pl.ds(0, 16), pl.ds(0, WIDTH)), (pl.ds(32, 16), pl.ds(256, WIDTH)))
     send_sib = copy(0, own, sib, sibling)
-    send_gx = copy(1, my_edge, gx_in.at[0], across)
-    send_gy = [copy(2 + s, own.at[:, toward[s]], gy_in.at[1 - s, 0], beside[s]) for s in range(2)]
-    send_co = [
-        copy(4 + s, own.at[pl.ds(edge, 16), toward[s]], co_in.at[1 - s, 0], corner[s])
+    send_gx = copy(1, slab, gx_in.at[0], across)
+    send_gy = [copy(2 + s, own.at[:, toward[s]], gy_in.at[1 - s, 0], beside[s][0]) for s in range(2)]
+    pass_gx = copy(4, gx_in.at[0], gx_in.at[1], sibling)
+    pass_gy = [copy(5 + s, gy_in.at[s, 0], gy_in.at[s, 1], sibling) for s in range(2)]
+    pass_co = [
+        [
+            copy(7 + 2 * s + c, gx_in.at[0, *inside[s]], co_in.at[1 - s, c], beside[s][c])
+            for c in range(2)
+        ]
         for s in range(2)
     ]
-    pass_gx = copy(6, gx_in.at[0], gx_in.at[1], sibling)
-    pass_gy = [copy(7 + s, gy_in.at[s, 0], gy_in.at[s, 1], sibling) for s in range(2)]
-    pass_co = [copy(9 + s, co_in.at[s, 0], co_in.at[s, 1], sibling) for s in range(2)]
 
     def arrived(number, dst):
         copy(number, dst, dst, sibling).wait_recv()
 
+    both_sides(lambda s: send_gy[s].start())
     send_gx.start()
-    both_sides(lambda s: send_co[s].start())
-    both_sides(lambda s: send_gy[s].start())
     send_sib.start()
 
     for side in range(2):
@@ -211,6 +232,7 @@
         def _(side=side):
             gy_in[side] = jnp.zeros(gy_in.shape[1:], BF16)
             co_in[side] = jnp.zeros(co_in.shape[1:], BF16)
+            take_co[side] = jnp.zeros(take_co.shape[1:], BF16)
 
     def column(row, col):
         col = jnp.minimum(jnp.maximum(col, 0), n_gy - 1)
@@ -239,7 +261,7 @@
     f_co = [[factors(e, exists[s]) for e in column(1 - i, j + 2 * s - 1)] for s in range(2)]
     live = valid.astype(F32)
 
-    build_weights(ps, i, wb, wbt, wc, wct, wa, wat)
+    build_forward(ps, wb, wc)
 
     def place(first_row, count, pair, mid, mix):
         mid_f[pl.ds(first_row * STEP_F + pair, count, stride=STEP_F), :] = mid
@@ -267,6 +289,7 @@
             arrived(3 - side, gy_in.at[side, 0])
             pass_gy[side].start()
 
+    build_rest(ps, i, wbt, wct, wa, wat)
     send_sib.wait_recv()
 
     @pl.loop(0, 32)
@@ -314,32 +337,45 @@
                 start = view * 32 * STEP_T + term * SPAN_A + chunk * CHUNK + a
                 t2[pl.ds(start, 32, stride=STEP_T), :] = second[a * 32 : a * 32 + 32, :]
 
-    pl.loop(0, 64 // CHUNK)(forward_chunk)
+    pl.loop(0, 2)(forward_chunk)
 
     arrived(1, gx_in.at[0])
     pass_gx.start()
+
+    def pass_ends(side):
+        for core in range(2):
+            pass_co[side][core].start()
+
+    both_sides(pass_ends)
+    pl.loop(2, 64 // CHUNK)(forward_chunk)
+
+    pass_gx.wait_recv()
     for side in range(2):
 
         @pl.when(exists[side])
         def _(side=side):
-            arrived(5 - side, co_in.at[side, 0])
-            pass_co[side].start()
-
-    pass_gx.wait_recv()
-    both_sides(lambda s: pass_co[s].wait_recv())
-
-    @pl.loop(0, 32)
-    def _(pair):
-        mid, mix = blend([gx_in[k, :, tile(pair)] for k in range(2)], f_gx)
-        place(64, 16, pair, mid, mix)
+            for core in range(2):
+                arrived(7 + 2 * (1 - side) + core, co_in.at[side, core])
+
+    def lengthen(rows):
+        return jnp.concatenate([rows, jnp.zeros((16 - HALO, rows.shape[1]), F32)], axis=0)
+
+    for q in range(4):
+        rows = [gx_in[k].astype(F32)[HALO * q : HALO * q + HALO] for k in range(2)]
+        for number in range(8):
+            lanes = slice(number * LANES, (number + 1) * LANES)
+            mid, mix = blend([lengthen(rows[k][:, lanes]) for k in range(2)], f_gx)
+            place(64, 16, q * 8 + number, mid, mix)
 
     for side in range(2):
+        down = 1 - side
         for pair in range(6):
-            lanes = pl.ds(pair * LANES, LANES)
-            mid, mix = blend([co_in[side, k, :, lanes] for k in range(2)], f_co[side])
+            lanes = slice(pair * LANES, (pair + 1) * LANES)
+            rows = [co_in[side, k, :, lanes].astype(F32)[down : down + HALO] for k in range(2)]
+            mid, mix = blend([lengthen(r) for r in rows], f_co[side])
             place(64, 16, first_pair[side] + pair, mid, mix)
 
-    pl.loop(64 // CHUNK, SPAN_A // CHUNK)(forward_chunk)
+    forward_chunk(64 // CHUNK)
     load_data.wait()
 
     def turn(step):
@@ -384,84 +420,135 @@
         at = pl.ds(first_row * STEP_F + pair, count, stride=STEP_F)
         return mid_f[at, :], mix_f[at, :]
 
-    pl.loop(64 // DUO, SPAN_A // DUO)(adjoint_rows)
-
-    @pl.loop(0, 32)
-    def _(pair):
-        mid, mix = fetch(64, 16, pair)
-        keep_gx[:, tile(pair)] = mid * f_gx[0][0] + mix * f_gx[0][1]
-        give_gx[:, tile(pair)] = (mid * f_gx[1][0] + mix * f_gx[1][1]).astype(BF16)
+    adjoint_rows(64 // DUO)
+    for q in range(4):
+        for number in range(8):
+            lanes = slice(number * LANES, (number + 1) * LANES)
+            mid, mix = fetch(64, 16, q * 8 + number)
+            mid, mix = mid[:HALO], mix[:HALO]
+            keep_gx[HALO * q : HALO * q + HALO, lanes] = mid * f_gx[0][0] + mix * f_gx[0][1]
+            part_gx[HALO * q : HALO * q + HALO, lanes] = mid * f_gx[1][0] + mix * f_gx[1][1]
+    keep_gx[44:48, :] = jnp.zeros((4, QUARTER), F32)
+    part_gx[44:48, :] = jnp.zeros((4, QUARTER), F32)
+    give_gx[...] = part_gx[...].astype(BF16)
+    share_gx = copy(11, give_gx, take_gx, sibling)
+    share_gx.start()
 
     for side in range(2):
+        down = 1 - side
         for pair in range(6):
+            lanes = slice(pair * LANES, (pair + 1) * LANES)
+            mid, mix = fetch(64, 16, first_pair[side] + pair)
+            for core in range(2):
+                factor = f_co[side][core]
+                rows = (mid * factor[0] + mix * factor[1])[:HALO]
+                parts = [jnp.zeros((down, LANES), F32)] if down else []
+                parts += [rows, jnp.zeros((16 - HALO - down, LANES), F32)]
+                give_co[side, core, :, lanes] = jnp.concatenate(parts, axis=0).astype(BF16)
+
+    send_co = [
+        [
+            copy(12 + 2 * s + c, give_co.at[s, c], take_co.at[1 - s, c], beside[s][c])
+            for c in range(2)
+        ]
+        for s in range(2)
+    ]
+
+    def send_ends(side):
+        for core in range(2):
+            send_co[side][core].start()
+
+    both_sides(send_ends)
+    final_gx = copy(16, put_gx, get_gx, across)
+
+    def finish_gx():
+        share_gx.wait_recv()
+        keep_gx[...] = keep_gx[...] + take_gx[...].astype(F32)
+        for side in range(2):
+
+            @pl.when(exists[side])
+            def _(side=side):
+                for core in range(2):
+                    arrived(12 + 2 * (1 - side) + core, take_co.at[side, core])
+
+        for side in range(2):
+            ends = take_co[side, 0].astype(F32) + take_co[side, 1].astype(F32)
+            keep_gx[inside[side]] = keep_gx[inside[side]] + ends
+        put_gx[...] = keep_gx[...].astype(BF16)
+        final_gx.start()
+
+    share_gy = [copy(17 + k, give_gy.at[k], take_gy.at[k], sibling) for k in range(4)]
+    final_gy = [
+        [
+            copy(21 + 2 * k + s, put_gy.at[k, s], get_gy.at[k, 1 - s], beside[s][0])
+            for s in range(2)
+        ]
+        for k in range(4)
+    ]
+    share_own = [
+        copy(29 + k, give_own.at[pl.ds(16 * k, 16)], take_own.at[pl.ds(16 * k, 16)], sibling)
+        for k in range(4)
+    ]
+
+    def own_rows(k):
+        adjoint_rows(k)
+        for side in range(2):
+            for pair in range(6):
+                lanes = pl.ds(pair * LANES, LANES)
+                mid, mix = fetch(16 * k, 16, first_pair[side] + pair)
+                one, two = f_gy[side]
+                keep_gy[k, side, :, lanes] = mid * one[0] + mix * one[1]
+                give_gy[k, side, :, lanes] = (mid * two[0] + mix * two[1]).astype(BF16)
+        share_gy[k].start()
+        for pair in range(32):
             lanes = pl.ds(pair * LANES, LANES)
-            mid, mix = fetch(64, 16, first_pair[side] + pair)
-            one, two = f_co[side]
-            keep_co[side, :, lanes] = mid * one[0] + mix * one[1]
-            give_co[side, :, lanes] = (mid * two[0] + mix * two[1]).astype(BF16)
-
-    share_gx = copy(11, give_gx, take_gx, sibling)
-    share_co = copy(12, give_co, take_co, sibling)
-    share_gx.start()
-    share_co.start()
-    pl.loop(0, 16 // DUO)(adjoint_rows)
-    share_gx.wait_recv()
-    share_co.wait_recv()
-    put_gx[...] = (keep_gx[...] + take_gx[...].astype(F32)).astype(BF16)
-    put_co[...] = (keep_co[...] + take_co[...].astype(F32)).astype(BF16)
-    final_gx = copy(13, put_gx, get_gx, across)
-    final_co = [copy(14 + s, put_co.at[s], get_co.at[1 - s], corner[s]) for s in range(2)]
-    final_gx.start()
-    both_sides(lambda s: final_co[s].start())
-    pl.loop(16 // DUO, 64 // DUO)(adjoint_rows)
-
-    for side in range(2):
-        for pair in range(6):
-            lanes = pl.ds(pair * LANES, LANES)
-            mid, mix = fetch(0, 64, first_pair[side] + pair)
-            one, two = f_gy[side]
-            keep_gy[side, :, lanes] = mid * one[0] + mix * one[1]
-            give_gy[side, :, lanes] = (mid * two[0] + mix * two[1]).astype(BF16)
-
-    share_gy = copy(16, give_gy, take_gy, sibling)
-    share_gy.start()
-
-    @pl.loop(0, 32)
-    def _(pair):
-        mid, mix = fetch(0, 64, pair)
-        out[0, :, tile(pair)] = mid
-        give_own[:, tile(pair)] = (mix * f_sib[1]).astype(BF16)
-
-    share_own = copy(17, give_own, take_own, sibling)
-    share_own.start()
-    share_gy.wait_recv()
-    put_gy[...] = (keep_gy[...] + take_gy[...].astype(F32)).astype(BF16)
-    final_gy = [copy(18 + s, put_gy.at[s], get_gy.at[1 - s], beside[s]) for s in range(2)]
-    both_sides(lambda s: final_gy[s].start())
-
-    share_own.wait_recv()
+            mid, mix = fetch(16 * k, 16, pair)
+            out[0, 16 * k : 16 * k + 16, lanes] = mid
+            give_own[16 * k : 16 * k + 16, lanes] = (mix * f_sib[1]).astype(BF16)
+        share_own[k].start()
+
+    def finish_gy(k):
+        share_gy[k].wait_recv()
+        put_gy[k] = (keep_gy[k] + take_gy[k].astype(F32)).astype(BF16)
+        both_sides(lambda s: final_gy[k][s].start())
+
+    own_rows(0)
+    finish_gx()
+    for k in range(1, 4):
+        own_rows(k)
+        finish_gy(k - 1)
+    finish_gy(3)
+
+    for k in range(4):
+        share_own[k].wait_recv()
     out[0] = out[0] + take_own[...].astype(F32)
     final_gx.wait_recv()
-    out[0, pl.ds(edge, 16), :] = out[0, pl.ds(edge, 16), :] + get_gx[...].astype(F32)
+    for q in range(4):
+        rows = get_gx[...].astype(F32)[HALO * q : HALO * q + HALO]
+        gap = jnp.zeros((16 - HALO, QUARTER), F32)
+        lanes = pl.ds(q * QUARTER, QUARTER)
+        out[0, 0:16, lanes] = out[0, 0:16, lanes] + jnp.concatenate([rows, gap], axis=0) * row
+        out[0, 48:64, lanes] = out[0, 48:64, lanes] + jnp.concatenate([gap, rows], axis=0) * (
+            1.0 - row
+        )
     for side in range(2):
 
         @pl.when(exists[side])
         def _(side=side):
-            arrived(15 - side, get_co.at[side])
-            arrived(19 - side, get_gy.at[side])
-            out[0, :, toward[side]] = out[0, :, toward[side]] + get_gy[side].astype(F32)
-            out[0, pl.ds(edge, 16), toward[side]] = out[0, pl.ds(edge, 16), toward[side]] + get_co[
-                side
-            ].astype(F32)
+            for k in range(4):
+                arrived(21 + 2 * k + 1 - side, get_gy.at[k, side])
+                rows = slice(16 * k, 16 * k + 16)
+                out[0, rows, toward[side]] = out[0, rows, toward[side]] + get_gy[k, side].astype(F32)
 
     out[0] = est[...] * out[0] * (live / VIEWS)
 
-    for item in (send_sib, send_gx, pass_gx, share_gx, share_co, final_gx, share_gy, share_own):
+    for item in [send_sib, send_gx, pass_gx, share_gx, final_gx] + share_gy + share_own:
         item.wait_send()
 
     def drain(side):
-        for group in (send_gy, send_co, pass_gy, pass_co, final_co, final_gy):
-            group[side].wait_send()
+        items = [send_gy[side], pass_gy[side], *pass_co[side], *send_co[side]]
+        for item in items + [final_gy[k][side] for k in range(4)]:
+            item.wait_send()
 
     both_sides(drain)
 
@@ -470,15 +557,17 @@
     n_gy = mesh.shape["gy"]
 
     def body(estimate, views_data, point_spread, block_owner):
-        slab, side, small = (16, 4096), (2, 64, WIDTH), (2, 16, WIDTH)
+        slab, ends = (48, QUARTER), (2, 2, 16, WIDTH)
+        sides = (4, 2, 16, WIDTH)
         scratch = [
             ((64, 4096), F32),
             ((VIEWS, 64, 4096), BF16),
             ((64, 4096), BF16),
             ((64, 4096), BF16),
-            ((2, 16, 4096), BF16),
+            (slab, BF16),
+            ((2, *slab), BF16),
             ((2, 2, 64, WIDTH), BF16),
-            ((2, 2, 16, WIDTH), BF16),
+            (ends, BF16),
             ((SPAN_A * STEP_F, LANES), F32),
             ((SPAN_A * STEP_F, LANES), F32),
             ((512, CHUNK * LANES), BF16),
@@ -491,22 +580,20 @@
             ((VIEWS, 64, 2 * SPAN_A), BF16),
             ((VIEWS, 2 * SPAN_A, 64), BF16),
             (slab, F32),
-            (side, F32),
-            (small, F32),
+            (slab, F32),
+            (sides, F32),
             ((64, 4096), BF16),
             (slab, BF16),
-            (side, BF16),
-            (small, BF16),
+            (sides, BF16),
+            (ends, BF16),
             ((64, 4096), BF16),
             (slab, BF16),
-            (side, BF16),
-            (small, BF16),
+            (sides, BF16),
+            (ends, BF16),
             (slab, BF16),
-            (side, BF16),
-            (small, BF16),
+            (sides, BF16),
             (slab, BF16),
-            (side, BF16),
-            (small, BF16),
+            (sides, BF16),
         ]
         any_spec = pl.BlockSpec(memory_space=pl.ANY)
         smem = pl.BlockSpec(memory_space=pltpu.SMEM)
@@ -518,8 +605,8 @@
             scratch_shapes=[pltpu.VMEM(shape, kind) for shape, kind in scratch]
             + [
                 pltpu.SemaphoreType.DMA((2,)),
-                pltpu.SemaphoreType.DMA((20,)),
-                pltpu.SemaphoreType.DMA((20,)),
+                pltpu.SemaphoreType.DMA((33,)),
+                pltpu.SemaphoreType.DMA((33,)),
             ],
             compiler_params=pltpu.CompilerParams(
                 collective_id=0, has_side_effects=True, vmem_limit_bytes=60 * 2**20

time: 60 us -> 56.9 us (0.948)
  the two profiles are of different devices: /device:TPU:33 before, /device:TPU:30 now
where the time goes in v2:
time: 56.9 us; the launch traced here: 56.7 us
  Pallas kernels  54.4 us (96%)
  local copies, waits for them, and re-layouts  2.27 us (4%)
    pallas_call x1, Pallas kernels, body(): pl.pallas_call(functools.partial(kernel, n_gy), out_shape=jax.ShapeDtypeS...  54.4 us
    unnamed x1, local copies, waits for them, and re-layouts  2.27 us

profile of v2, /device:TPU:30, one launch (start us, length us, event | category | flops | bytes accessed | tf_op | source)
XLA Modules:
  0.0 56.7 jit_solution(12834402628189228449)
XLA Ops:
  0.0 54.4 %shard_map.46 = f32[1,64,4096]{2,1,0:T(8,128)} custom-call(f32[1,64,4096]{2,1,0:T(8,128)} %est_hbm.1, bf16[4,1,64,4096]{3,2,1,0:T(8,128)(2,1)} %data_hbm.1, f32[4,3,2,23]{3,2,1,0:T(2,128)} %bitcast.2, s32[2,4,64]{2,1,0:T(4,128)} %bitcast.3), custom_call_target="tpu_custom_call" | custom-call | tf_op jit(solution)/shard_map/pallas_call | solution.py:600
  54.4 2.3 %copy.6 = f32[1,64,4096]{2,1,0:T(8,128)} copy(f32[1,64,4096]{2,1,0:T(8,128)} %shard_map.46) | data formatting | bytes 2097152

commit v3 on v2

--- a/solution.py
+++ b/solution.py
@@ -18,7 +18,6 @@
 WIDTH = 768
 FACE = 3328
 QUARTER = 1024
-TURN = 32
 CHUNK = 16
 DUO = 16
 
@@ -71,7 +70,7 @@
         wc[number, 128:256, :] = jnp.where(lane >= 64, base, 0.0).astype(BF16)
 
 
-def build_rest(ps, mesh_row, wbt, wct, wa, wat):
+def build_rest(ps, mesh_row, wbt, wct, wa, wat_own, wat_far):
     tap = tap_of(ps)
     d_ct = ext_c(iota((64, LANES), 1)) - iota((64, LANES), 0) + HALO
     wct[...] = jnp.zeros_like(wct)
@@ -104,8 +103,10 @@
     def _(view):
         first_tap, second_tap = tap(2 * view, 0), tap(2 * view + 1, 0)
         wa[view] = band(d_a, lambda t: jnp.where(second, second_tap(t), first_tap(t))).astype(BF16)
-        wat[view, 0:SPAN_A, :] = band(d_at, first_tap).astype(BF16)
-        wat[view, SPAN_A : 2 * SPAN_A, :] = band(d_at, second_tap).astype(BF16)
+        for term, taps in enumerate((first_tap, second_tap)):
+            base = band(d_at, taps).astype(BF16)
+            wat_own[view, term * 64 : term * 64 + 64, :] = base[:64]
+            wat_far[view, term * 16 : term * 16 + 16, :] = base[64:]
 
 
 def kernel(
@@ -133,10 +134,10 @@
     wc,
     wct,
     wa,
-    wat,
+    wat_own,
+    wat_far,
     keep_gx,
     part_gx,
-    keep_gy,
     give_own,
     give_gx,
     give_gy,
@@ -146,9 +147,7 @@
     take_gy,
     take_co,
     put_gx,
-    put_gy,
     get_gx,
-    get_gy,
     load_sem,
     send_sem,
     recv_sem,
@@ -159,9 +158,15 @@
     beside = [[(i, j + 2 * s - 1, g), (i, j + 2 * s - 1, 1 - g)] for s in range(2)]
     exists = (j > 0, j < n_gy - 1)
 
-    load_est = pltpu.make_async_copy(est_hbm.at[0], est, load_sem.at[0])
-    load_data = pltpu.make_async_copy(data_hbm.at[:, 0], data, load_sem.at[1])
-    load_est.start()
+    toward = (pl.ds(0, WIDTH), pl.ds(FACE, WIDTH))
+    parts = (*toward, pl.ds(WIDTH, FACE - WIDTH))
+    load_est = [
+        pltpu.make_async_copy(est_hbm.at[0, :, p], est.at[:, p], load_sem.at[n])
+        for n, p in enumerate(parts)
+    ]
+    load_data = pltpu.make_async_copy(data_hbm.at[:, 0], data, load_sem.at[3])
+    for item in load_est:
+        item.start()
     load_data.start()
 
     def copy(number, src, dst, target):
@@ -192,19 +197,12 @@
             )
 
     both_sides(greet)
-    load_est.wait()
-    own[...] = est[...].astype(BF16)
-
-    row = i.astype(F32)
-    edge = est[53:64, :] * (1.0 - row) + est[0:HALO, :] * row
-    slab[...] = jnp.concatenate(
-        [edge[:, q * QUARTER : (q + 1) * QUARTER] for q in range(4)] + [jnp.zeros((4, QUARTER), F32)],
-        axis=0,
-    ).astype(BF16)
+    for item, lanes in zip(load_est[:2], toward):
+        item.wait()
+        own[:, lanes] = est[:, lanes].astype(BF16)
     waits = 2 + 2 * exists[0].astype(I32) + 2 * exists[1].astype(I32)
     pl.semaphore_wait(barrier, waits)
 
-    toward = (pl.ds(0, WIDTH), pl.ds(FACE, WIDTH))
     inside = ((pl.ds(0, 16), pl.ds(0, WIDTH)), (pl.ds(32, 16), pl.ds(256, WIDTH)))
     send_sib = copy(0, own, sib, sibling)
     send_gx = copy(1, slab, gx_in.at[0], across)
@@ -223,8 +221,16 @@
         copy(number, dst, dst, sibling).wait_recv()
 
     both_sides(lambda s: send_gy[s].start())
-    send_gx.start()
+    load_est[2].wait()
+    own[:, parts[2]] = est[:, parts[2]].astype(BF16)
     send_sib.start()
+
+    row = i.astype(F32)
+    edge = est[53:64, :] * (1.0 - row) + est[0:HALO, :] * row
+    slab[...] = jnp.concatenate(
+        [edge[:, q * QUARTER : (q + 1) * QUARTER] for q in range(4)] + [jnp.zeros((4, QUARTER), F32)],
+        axis=0,
+    ).astype(BF16)
 
     for side in range(2):
 
@@ -262,6 +268,7 @@
     live = valid.astype(F32)
 
     build_forward(ps, wb, wc)
+    send_gx.start()
 
     def place(first_row, count, pair, mid, mix):
         mid_f[pl.ds(first_row * STEP_F + pair, count, stride=STEP_F), :] = mid
@@ -289,7 +296,7 @@
             arrived(3 - side, gy_in.at[side, 0])
             pass_gy[side].start()
 
-    build_rest(ps, i, wbt, wct, wa, wat)
+    build_rest(ps, i, wbt, wct, wa, wat_own, wat_far)
     send_sib.wait_recv()
 
     @pl.loop(0, 32)
@@ -378,30 +385,34 @@
     forward_chunk(64 // CHUNK)
     load_data.wait()
 
-    def turn(step):
-        view, group = step // (32 // TURN), step % (32 // TURN)
-        start = pl.multiple_of((view * 32 + group * TURN) * STEP_T, 8)
+    def adjoint_front(view, back, count, first):
+        for term in range(RANK):
+            rows = back[term * count : (term + 1) * count]
+            block = jnp.concatenate([rows[:, k * LANES : (k + 1) * LANES] for k in range(32)], axis=0)
+            wide = jnp.dot(block, wct[view * RANK + term], preferred_element_type=F32)
+            for k in range(32):
+                for odd in range(2):
+                    at = first * STEP_V + (view * RANK + term) * 64 + odd * 32 + k
+                    v2[pl.ds(at, count, stride=STEP_V), :] = wide[
+                        k * count : (k + 1) * count, odd * LANES : (odd + 1) * LANES
+                    ]
+
+    def turn_far(view):
+        start = pl.multiple_of(view * 32 * STEP_T, 8)
         fields = jnp.concatenate(
-            [t2[pl.ds(start + k * STEP_T, 2 * SPAN_A), :].astype(BF16) for k in range(TURN)], axis=1
+            [t2[pl.ds(start + k * STEP_T, 2 * SPAN_A), :].astype(BF16) for k in range(32)], axis=1
         )
         blurred = jnp.dot(wa[view], fields, preferred_element_type=F32)
-        lanes = pl.ds(pl.multiple_of(group * (TURN * LANES), TURN * LANES), TURN * LANES)
-        ratio = (data[view, :, lanes].astype(F32) / jnp.maximum(blurred, FLOOR) * live).astype(BF16)
-        back = jnp.dot(wat[view], ratio, preferred_element_type=F32).astype(BF16)
-        for term in range(RANK):
-            rows = back[term * SPAN_A : (term + 1) * SPAN_A]
-            block = jnp.concatenate(
-                [rows[:, k * LANES : (k + 1) * LANES] for k in range(TURN)], axis=0
-            )
-            wide = jnp.dot(block, wct[view * RANK + term], preferred_element_type=F32)
-            for k in range(TURN):
-                for odd in range(2):
-                    at = (view * RANK + term) * 64 + odd * 32 + group * TURN + k
-                    v2[pl.ds(at, SPAN_A, stride=STEP_V), :] = wide[
-                        k * SPAN_A : (k + 1) * SPAN_A, odd * LANES : (odd + 1) * LANES
-                    ]
-
-    pl.loop(0, VIEWS * 32 // TURN)(turn)
+        ratio = (data[view].astype(F32) / jnp.maximum(blurred, FLOOR) * live).astype(BF16)
+        data[view] = ratio
+        back = jnp.dot(wat_far[view], ratio, preferred_element_type=F32).astype(BF16)
+        adjoint_front(view, back, 16, 64)
+
+    def turn_own(view):
+        back = jnp.dot(wat_own[view], data[view], preferred_element_type=F32).astype(BF16)
+        adjoint_front(view, back, 64, 0)
+
+    pl.loop(0, VIEWS)(turn_far)
 
     def adjoint_rows(step):
         start = pl.multiple_of(step * DUO * STEP_V, 8)
@@ -477,16 +488,23 @@
         put_gx[...] = keep_gx[...].astype(BF16)
         final_gx.start()
 
-    share_gy = [copy(17 + k, give_gy.at[k], take_gy.at[k], sibling) for k in range(4)]
-    final_gy = [
+    pl.loop(0, VIEWS // 2)(turn_own)
+    finish_gx()
+    pl.loop(VIEWS // 2, VIEWS)(turn_own)
+
+    scale = live / VIEWS
+    send_sides = [
         [
-            copy(21 + 2 * k + s, put_gy.at[k, s], get_gy.at[k, 1 - s], beside[s][0])
+            [
+                copy(17 + 4 * k + 2 * s + c, give_gy.at[k, s, c], take_gy.at[k, 1 - s, c], beside[s][c])
+                for c in range(2)
+            ]
             for s in range(2)
         ]
         for k in range(4)
     ]
     share_own = [
-        copy(29 + k, give_own.at[pl.ds(16 * k, 16)], take_own.at[pl.ds(16 * k, 16)], sibling)
+        copy(33 + k, give_own.at[pl.ds(16 * k, 16)], take_own.at[pl.ds(16 * k, 16)], sibling)
         for k in range(4)
     ]
 
@@ -496,10 +514,15 @@
             for pair in range(6):
                 lanes = pl.ds(pair * LANES, LANES)
                 mid, mix = fetch(16 * k, 16, first_pair[side] + pair)
-                one, two = f_gy[side]
-                keep_gy[k, side, :, lanes] = mid * one[0] + mix * one[1]
-                give_gy[k, side, :, lanes] = (mid * two[0] + mix * two[1]).astype(BF16)
-        share_gy[k].start()
+                for core in range(2):
+                    factor = f_gy[side][core]
+                    give_gy[k, side, core, :, lanes] = (mid * factor[0] + mix * factor[1]).astype(BF16)
+
+        def send(side):
+            for core in range(2):
+                send_sides[k][side][core].start()
+
+        both_sides(send)
         for pair in range(32):
             lanes = pl.ds(pair * LANES, LANES)
             mid, mix = fetch(16 * k, 16, pair)
@@ -507,47 +530,45 @@
             give_own[16 * k : 16 * k + 16, lanes] = (mix * f_sib[1]).astype(BF16)
         share_own[k].start()
 
-    def finish_gy(k):
-        share_gy[k].wait_recv()
-        put_gy[k] = (keep_gy[k] + take_gy[k].astype(F32)).astype(BF16)
-        both_sides(lambda s: final_gy[k][s].start())
+    def finish_own(k):
+        share_own[k].wait_recv()
+        rows = slice(16 * k, 16 * k + 16)
+        out[0, rows] = (out[0, rows] + take_own[rows].astype(F32)) * (est[rows] * scale)
 
     own_rows(0)
-    finish_gx()
     for k in range(1, 4):
         own_rows(k)
-        finish_gy(k - 1)
-    finish_gy(3)
-
-    for k in range(4):
-        share_own[k].wait_recv()
-    out[0] = out[0] + take_own[...].astype(F32)
+        finish_own(k - 1)
+    finish_own(3)
+
     final_gx.wait_recv()
     for q in range(4):
         rows = get_gx[...].astype(F32)[HALO * q : HALO * q + HALO]
         gap = jnp.zeros((16 - HALO, QUARTER), F32)
         lanes = pl.ds(q * QUARTER, QUARTER)
-        out[0, 0:16, lanes] = out[0, 0:16, lanes] + jnp.concatenate([rows, gap], axis=0) * row
-        out[0, 48:64, lanes] = out[0, 48:64, lanes] + jnp.concatenate([gap, rows], axis=0) * (
-            1.0 - row
-        )
-    for side in range(2):
-
-        @pl.when(exists[side])
-        def _(side=side):
-            for k in range(4):
-                arrived(21 + 2 * k + 1 - side, get_gy.at[k, side])
+        low_rows = jnp.concatenate([rows, gap], axis=0) * (row * scale)
+        high_rows = jnp.concatenate([gap, rows], axis=0) * ((1.0 - row) * scale)
+        out[0, 0:16, lanes] = out[0, 0:16, lanes] + low_rows * est[0:16, lanes]
+        out[0, 48:64, lanes] = out[0, 48:64, lanes] + high_rows * est[48:64, lanes]
+    for k in range(4):
+        for side in range(2):
+
+            @pl.when(exists[side])
+            def _(k=k, side=side):
+                for core in range(2):
+                    arrived(17 + 4 * k + 2 * (1 - side) + core, take_gy.at[k, side, core])
                 rows = slice(16 * k, 16 * k + 16)
-                out[0, rows, toward[side]] = out[0, rows, toward[side]] + get_gy[k, side].astype(F32)
-
-    out[0] = est[...] * out[0] * (live / VIEWS)
-
-    for item in [send_sib, send_gx, pass_gx, share_gx, final_gx] + share_gy + share_own:
+                total = take_gy[k, side, 0].astype(F32) + take_gy[k, side, 1].astype(F32)
+                out[0, rows, toward[side]] = out[0, rows, toward[side]] + total * (
+                    est[rows, toward[side]] * scale
+                )
+
+    for item in [send_sib, send_gx, pass_gx, share_gx, final_gx] + share_own:
         item.wait_send()
 
     def drain(side):
         items = [send_gy[side], pass_gy[side], *pass_co[side], *send_co[side]]
-        for item in items + [final_gy[k][side] for k in range(4)]:
+        for item in items + [c for k in range(4) for c in send_sides[k][side]]:
             item.wait_send()
 
     both_sides(drain)
@@ -558,7 +579,7 @@
 
     def body(estimate, views_data, point_spread, block_owner):
         slab, ends = (48, QUARTER), (2, 2, 16, WIDTH)
-        sides = (4, 2, 16, WIDTH)
+        sides = (4, 2, 2, 16, WIDTH)
         scratch = [
             ((64, 4096), F32),
             ((VIEWS, 64, 4096), BF16),
@@ -578,10 +599,10 @@
             ((8, 256, 128), BF16),
             ((8, 128, 256), BF16),
             ((VIEWS, 64, 2 * SPAN_A), BF16),
-            ((VIEWS, 2 * SPAN_A, 64), BF16),
+            ((VIEWS, RANK * 64, 64), BF16),
+            ((VIEWS, RANK * 16, 64), BF16),
             (slab, F32),
             (slab, F32),
-            (sides, F32),
             ((64, 4096), BF16),
             (slab, BF16),
             (sides, BF16),
@@ -591,9 +612,7 @@
             (sides, BF16),
             (ends, BF16),
             (slab, BF16),
-            (sides, BF16),
             (slab, BF16),
-            (sides, BF16),
         ]
         any_spec = pl.BlockSpec(memory_space=pl.ANY)
         smem = pl.BlockSpec(memory_space=pltpu.SMEM)
@@ -604,9 +623,9 @@
             out_specs=pl.BlockSpec(memory_space=pltpu.VMEM),
             scratch_shapes=[pltpu.VMEM(shape, kind) for shape, kind in scratch]
             + [
-                pltpu.SemaphoreType.DMA((2,)),
-                pltpu.SemaphoreType.DMA((33,)),
-                pltpu.SemaphoreType.DMA((33,)),
+                pltpu.SemaphoreType.DMA((4,)),
+                pltpu.SemaphoreType.DMA((37,)),
+                pltpu.SemaphoreType.DMA((37,)),
             ],
             compiler_params=pltpu.CompilerParams(
                 collective_id=0, has_side_effects=True, vmem_limit_bytes=60 * 2**20

time: 56.9 us -> 55 us (0.967)
  the two profiles are of different devices: /device:TPU:30 before, /device:TPU:33 now
where the time goes in v3:
time: 55 us; the launch traced here: 54.8 us
  Pallas kernels  52.6 us (96%)
  local copies, waits for them, and re-layouts  2.27 us (4%)
    pallas_call x1, Pallas kernels, body(): pl.pallas_call(functools.partial(kernel, n_gy), out_shape=jax.ShapeDtypeS...  52.6 us
    unnamed x1, local copies, waits for them, and re-layouts  2.27 us

profile of v3, /device:TPU:33, one launch (start us, length us, event | category | flops | bytes accessed | tf_op | source)
XLA Modules:
  0.0 54.8 jit_solution(18190178688926227700)
XLA Ops:
  0.0 52.6 %shard_map.46 = f32[1,64,4096]{2,1,0:T(8,128)} custom-call(f32[1,64,4096]{2,1,0:T(8,128)} %est_hbm.1, bf16[4,1,64,4096]{3,2,1,0:T(8,128)(2,1)} %data_hbm.1, f32[4,3,2,23]{3,2,1,0:T(2,128)} %bitcast.2, s32[2,4,64]{2,1,0:T(4,128)} %bitcast.3), custom_call_target="tpu_custom_call" | custom-call | tf_op jit(solution)/shard_map/pallas_call | solution.py:619
  52.6 2.3 %copy.6 = f32[1,64,4096]{2,1,0:T(8,128)} copy(f32[1,64,4096]{2,1,0:T(8,128)} %shard_map.46) | data formatting | bytes 2097152

commit v4 on v3

--- a/solution.py
+++ b/solution.py
@@ -268,6 +268,7 @@
     live = valid.astype(F32)
 
     build_forward(ps, wb, wc)
+    build_rest(ps, i, wbt, wct, wa, wat_own, wat_far)
     send_gx.start()
 
     def place(first_row, count, pair, mid, mix):
@@ -289,6 +290,12 @@
 
     first_pair = (38, 32)
 
+    send_sib.wait_recv()
+
+    @pl.loop(0, 32)
+    def _(pair):
+        place(0, 64, pair, own[:, tile(pair)].astype(F32), sib[:, tile(pair)].astype(F32) * f_sib[1])
+
     for side in range(2):
 
         @pl.when(exists[side])
@@ -296,12 +303,6 @@
             arrived(3 - side, gy_in.at[side, 0])
             pass_gy[side].start()
 
-    build_rest(ps, i, wbt, wct, wa, wat_own, wat_far)
-    send_sib.wait_recv()
-
-    @pl.loop(0, 32)
-    def _(pair):
-        place(0, 64, pair, own[:, tile(pair)].astype(F32), sib[:, tile(pair)].astype(F32) * f_sib[1])
 
     both_sides(lambda s: pass_gy[s].wait_recv())
     for side in range(2):
@@ -344,7 +345,7 @@
                 start = view * 32 * STEP_T + term * SPAN_A + chunk * CHUNK + a
                 t2[pl.ds(start, 32, stride=STEP_T), :] = second[a * 32 : a * 32 + 32, :]
 
-    pl.loop(0, 2)(forward_chunk)
+    pl.loop(0, 3)(forward_chunk)
 
     arrived(1, gx_in.at[0])
     pass_gx.start()
@@ -354,7 +355,7 @@
             pass_co[side][core].start()
 
     both_sides(pass_ends)
-    pl.loop(2, 64 // CHUNK)(forward_chunk)
+    forward_chunk(3)
 
     pass_gx.wait_recv()
     for side in range(2):
@@ -488,9 +489,9 @@
         put_gx[...] = keep_gx[...].astype(BF16)
         final_gx.start()
 
-    pl.loop(0, VIEWS // 2)(turn_own)
+    pl.loop(0, VIEWS - 1)(turn_own)
     finish_gx()
-    pl.loop(VIEWS // 2, VIEWS)(turn_own)
+    turn_own(VIEWS - 1)
 
     scale = live / VIEWS
     send_sides = [
@@ -523,6 +524,8 @@
                 send_sides[k][side][core].start()
 
         both_sides(send)
+
+    def own_block(k):
         for pair in range(32):
             lanes = pl.ds(pair * LANES, LANES)
             mid, mix = fetch(16 * k, 16, pair)
@@ -535,10 +538,12 @@
         rows = slice(16 * k, 16 * k + 16)
         out[0, rows] = (out[0, rows] + take_own[rows].astype(F32)) * (est[rows] * scale)
 
-    own_rows(0)
-    for k in range(1, 4):
+    for k in range(4):
         own_rows(k)
-        finish_own(k - 1)
+    for k in range(4):
+        own_block(k)
+        if k:
+            finish_own(k - 1)
     finish_own(3)
 
     final_gx.wait_recv()
@@ -628,7 +633,7 @@
                 pltpu.SemaphoreType.DMA((37,)),
             ],
             compiler_params=pltpu.CompilerParams(
-                collective_id=0, has_side_effects=True, vmem_limit_bytes=60 * 2**20
+                collective_id=0, has_side_effects=True, vmem_limit_bytes=52 * 2**20
             ),
         )(
             estimate,

time: 55 us -> 53.9 us (0.980)
  Pallas kernels: 52.6 us -> 51.4 us
    pallas_call x1, Pallas kernels: 52.6 us -> 51.4 us  [body(): pl.pallas_call(functools.partial(kernel, n_gy), out_shape=jax.ShapeDtypeS...]
    unnamed x1 -> x5, local copies, waits for them, and re-layouts: 2.27 us -> 2.37 us
where the time goes in v4:
time: 53.9 us; the launch traced here: 53.8 us
  Pallas kernels  51.4 us (95%)
  local copies, waits for them, and re-layouts  2.37 us (4%)
    pallas_call x1, Pallas kernels, body(): pl.pallas_call(functools.partial(kernel, n_gy), out_shape=jax.ShapeDtypeS...  51.4 us
    unnamed x5, local copies, waits for them, and re-layouts  2.37 us

profile of v4, /device:TPU:33, one launch (start us, length us, event | category | flops | bytes accessed | tf_op | source)
XLA Modules:
  0.0 53.8 jit_solution(14344765665108912430)
XLA Ops:
  0.0 0.0 copy-start
  0.0 0.7 %copy-done = f32[4,2,3,23]{3,1,2,0:T(2,128)S(1)} copy-done((f32[4,2,3,23]{3,1,2,0:T(2,128)S(1)}, f32[4,2,3,23]{3,1,2,0:T(2,128)}, u32[]{:S(2)}) %copy-start) | copy-done | bytes 2232
  0.7 0.0 copy-start.1
  0.7 0.7 %copy-done.1 = s32[2,64,4]{1,2,0:T(4,128)S(1)} copy-done((s32[2,64,4]{1,2,0:T(4,128)S(1)}, s32[2,64,4]{1,2,0:T(4,128)}, u32[]{:S(2)}) %copy-start.1) | copy-done | bytes 2072
  1.4 51.4 %shard_map.46 = f32[1,64,4096]{2,1,0:T(8,128)S(1)} custom-call(f32[1,64,4096]{2,1,0:T(8,128)} %est_hbm.1, bf16[4,1,64,4096]{3,2,1,0:T(8,128)(2,1)} %data_hbm.1, f32[4,3,2,23]{3,2,1,0:T(2,128)S(1)} %bitcast.2, s32[2,4,64]{2,1,0:T(4,128)S(1)} %bitcast.3), custom_call_target="tpu_custom_call" | custom-call | tf_op jit(solution)/shard_map/pallas_call | solution.py:624
  52.8 1.0 %copy.6 = f32[1,64,4096]{2,1,0:T(8,128)} copy(f32[1,64,4096]{2,1,0:T(8,128)S(1)} %shard_map.46) | data formatting | bytes 2097152
Async XLA Ops:
  0.0 0.7 %copy-start = (f32[4,2,3,23]{3,1,2,0:T(2,128)S(1)}, f32[4,2,3,23]{3,1,2,0:T(2,128)}, u32[]{:S(2)}) copy-start(f32[4,2,3,23]{3,1,2,0:T(2,128)} %param.6) | copy-start | bytes 6628
  0.7 0.7 %copy-start.1 = (s32[2,64,4]{1,2,0:T(4,128)S(1)}, s32[2,64,4]{1,2,0:T(4,128)}, u32[]{:S(2)}) copy-start(s32[2,64,4]{1,2,0:T(4,128)} %param.7) | copy-start | bytes 6148

commit v5 on v4

--- a/solution.py
+++ b/solution.py
@@ -206,9 +206,22 @@
     inside = ((pl.ds(0, 16), pl.ds(0, WIDTH)), (pl.ds(32, 16), pl.ds(256, WIDTH)))
     send_sib = copy(0, own, sib, sibling)
     send_gx = copy(1, slab, gx_in.at[0], across)
-    send_gy = [copy(2 + s, own.at[:, toward[s]], gy_in.at[1 - s, 0], beside[s][0]) for s in range(2)]
+    rows_of = [pl.ds(16 * k, 16) for k in range(4)]
+    send_gy = [
+        [
+            copy(37 + 2 * k + s, own.at[rows_of[k], toward[s]], gy_in.at[1 - s, 0, rows_of[k]], beside[s][0])
+            for s in range(2)
+        ]
+        for k in range(4)
+    ]
     pass_gx = copy(4, gx_in.at[0], gx_in.at[1], sibling)
-    pass_gy = [copy(5 + s, gy_in.at[s, 0], gy_in.at[s, 1], sibling) for s in range(2)]
+    pass_gy = [
+        [
+            copy(45 + 2 * k + s, gy_in.at[s, 0, rows_of[k]], gy_in.at[s, 1, rows_of[k]], sibling)
+            for s in range(2)
+        ]
+        for k in range(4)
+    ]
     pass_co = [
         [
             copy(7 + 2 * s + c, gx_in.at[0, *inside[s]], co_in.at[1 - s, c], beside[s][c])
@@ -220,7 +233,12 @@
     def arrived(number, dst):
         copy(number, dst, dst, sibling).wait_recv()
 
-    both_sides(lambda s: send_gy[s].start())
+
+    def send_rows(side):
+        for k in range(4):
+            send_gy[k][side].start()
+
+    both_sides(send_rows)
     load_est[2].wait()
     own[:, parts[2]] = est[:, parts[2]].astype(BF16)
     send_sib.start()
@@ -268,8 +286,8 @@
     live = valid.astype(F32)
 
     build_forward(ps, wb, wc)
+    send_gx.start()
     build_rest(ps, i, wbt, wct, wa, wat_own, wat_far)
-    send_gx.start()
 
     def place(first_row, count, pair, mid, mix):
         mid_f[pl.ds(first_row * STEP_F + pair, count, stride=STEP_F), :] = mid
@@ -296,20 +314,21 @@
     def _(pair):
         place(0, 64, pair, own[:, tile(pair)].astype(F32), sib[:, tile(pair)].astype(F32) * f_sib[1])
 
-    for side in range(2):
-
-        @pl.when(exists[side])
-        def _(side=side):
-            arrived(3 - side, gy_in.at[side, 0])
-            pass_gy[side].start()
-
-
-    both_sides(lambda s: pass_gy[s].wait_recv())
-    for side in range(2):
-        for pair in range(6):
-            lanes = pl.ds(pair * LANES, LANES)
-            mid, mix = blend([gy_in[side, k, :, lanes] for k in range(2)], f_gy[side])
-            place(0, 64, first_pair[side] + pair, mid, mix)
+    def hand_on(k):
+        for side in range(2):
+
+            @pl.when(exists[side])
+            def _(side=side):
+                arrived(37 + 2 * k + 1 - side, gy_in.at[side, 0, rows_of[k]])
+                pass_gy[k][side].start()
+
+    def select_rows(k):
+        both_sides(lambda s: pass_gy[k][s].wait_recv())
+        for side in range(2):
+            for pair in range(6):
+                lanes = pl.ds(pair * LANES, LANES)
+                mid, mix = blend([gy_in[side, c, rows_of[k], lanes] for c in range(2)], f_gy[side])
+                place(16 * k, 16, first_pair[side] + pair, mid, mix)
 
     low = iota((PAIRS, LANES), 1) < 64
 
@@ -345,7 +364,11 @@
                 start = view * 32 * STEP_T + term * SPAN_A + chunk * CHUNK + a
                 t2[pl.ds(start, 32, stride=STEP_T), :] = second[a * 32 : a * 32 + 32, :]
 
-    pl.loop(0, 3)(forward_chunk)
+    hand_on(0)
+    for k in range(3):
+        hand_on(k + 1)
+        select_rows(k)
+        forward_chunk(k)
 
     arrived(1, gx_in.at[0])
     pass_gx.start()
@@ -355,6 +378,7 @@
             pass_co[side][core].start()
 
     both_sides(pass_ends)
+    select_rows(3)
     forward_chunk(3)
 
     pass_gx.wait_recv()
@@ -572,8 +596,10 @@
         item.wait_send()
 
     def drain(side):
-        items = [send_gy[side], pass_gy[side], *pass_co[side], *send_co[side]]
-        for item in items + [c for k in range(4) for c in send_sides[k][side]]:
+        items = [*pass_co[side], *send_co[side]]
+        for k in range(4):
+            items += [send_gy[k][side], pass_gy[k][side], *send_sides[k][side]]
+        for item in items:
             item.wait_send()
 
     both_sides(drain)
@@ -619,18 +645,18 @@
             (slab, BF16),
             (slab, BF16),
         ]
-        any_spec = pl.BlockSpec(memory_space=pl.ANY)
+        far_spec = pl.BlockSpec(memory_space=pltpu.HBM)
         smem = pl.BlockSpec(memory_space=pltpu.SMEM)
         return pl.pallas_call(
             functools.partial(kernel, n_gy),
             out_shape=jax.ShapeDtypeStruct((1, 64, 4096), F32),
-            in_specs=[any_spec, any_spec, smem, smem],
+            in_specs=[far_spec, far_spec, smem, smem],
             out_specs=pl.BlockSpec(memory_space=pltpu.VMEM),
             scratch_shapes=[pltpu.VMEM(shape, kind) for shape, kind in scratch]
             + [
                 pltpu.SemaphoreType.DMA((4,)),
-                pltpu.SemaphoreType.DMA((37,)),
-                pltpu.SemaphoreType.DMA((37,)),
+                pltpu.SemaphoreType.DMA((53,)),
+                pltpu.SemaphoreType.DMA((53,)),
             ],
             compiler_params=pltpu.CompilerParams(
                 collective_id=0, has_side_effects=True, vmem_limit_bytes=52 * 2**20

time: 53.9 us -> 52.2 us (0.968)
  Pallas kernels: 51.4 us -> 49.7 us
    pallas_call x1, Pallas kernels: 51.4 us -> 49.7 us  [body(): pl.pallas_call(functools.partial(kernel, n_gy), out_shape=jax.ShapeDtypeS...]
where the time goes in v5:
time: 52.2 us; the launch traced here: 52 us
  Pallas kernels  49.7 us (95%)
  local copies, waits for them, and re-layouts  2.37 us (5%)
    pallas_call x1, Pallas kernels, body(): pl.pallas_call(functools.partial(kernel, n_gy), out_shape=jax.ShapeDtypeS...  49.7 us
    unnamed x5, local copies, waits for them, and re-layouts  2.37 us

profile of v5, /device:TPU:33, one launch (start us, length us, event | category | flops | bytes accessed | tf_op | source)
XLA Modules:
  0.0 52.0 jit_solution(4316245184932426443)
XLA Ops:
  0.0 0.0 copy-start
  0.0 0.7 %copy-done = f32[4,2,3,23]{3,1,2,0:T(2,128)S(1)} copy-done((f32[4,2,3,23]{3,1,2,0:T(2,128)S(1)}, f32[4,2,3,23]{3,1,2,0:T(2,128)}, u32[]{:S(2)}) %copy-start) | copy-done | bytes 2232
  0.7 0.0 copy-start.1
  0.7 0.7 %copy-done.1 = s32[2,64,4]{1,2,0:T(4,128)S(1)} copy-done((s32[2,64,4]{1,2,0:T(4,128)S(1)}, s32[2,64,4]{1,2,0:T(4,128)}, u32[]{:S(2)}) %copy-start.1) | copy-done | bytes 2072
  1.4 49.7 %shard_map.46 = f32[1,64,4096]{2,1,0:T(8,128)S(1)} custom-call(f32[1,64,4096]{2,1,0:T(8,128)} %est_hbm.1, bf16[4,1,64,4096]{3,2,1,0:T(8,128)(2,1)} %data_hbm.1, f32[4,3,2,23]{3,2,1,0:T(2,128)S(1)} %bitcast.2, s32[2,4,64]{2,1,0:T(4,128)S(1)} %bitcast.3), custom_call_target="tpu_custom_call" | custom-call | tf_op jit(solution)/shard_map/pallas_call | solution.py:650
  51.1 1.0 %copy.6 = f32[1,64,4096]{2,1,0:T(8,128)} copy(f32[1,64,4096]{2,1,0:T(8,128)S(1)} %shard_map.46) | data formatting | bytes 2097152
Async XLA Ops:
  0.0 0.7 %copy-start = (f32[4,2,3,23]{3,1,2,0:T(2,128)S(1)}, f32[4,2,3,23]{3,1,2,0:T(2,128)}, u32[]{:S(2)}) copy-start(f32[4,2,3,23]{3,1,2,0:T(2,128)} %param.6) | copy-start | bytes 6628
  0.7 0.7 %copy-start.1 = (s32[2,64,4]{1,2,0:T(4,128)S(1)}, s32[2,64,4]{1,2,0:T(4,128)}, u32[]{:S(2)}) copy-start(s32[2,64,4]{1,2,0:T(4,128)} %param.7) | copy-start | bytes 6148

commit v6 on v5

--- a/solution.py
+++ b/solution.py
@@ -113,8 +113,8 @@
     n_gy,
     est_hbm,
     data_hbm,
-    ps,
-    owner,
+    ps_hbm,
+    owner_hbm,
     out,
     est,
     data,
@@ -138,6 +138,7 @@
     wat_far,
     keep_gx,
     part_gx,
+    keep_co,
     give_own,
     give_gx,
     give_gy,
@@ -147,7 +148,11 @@
     take_gy,
     take_co,
     put_gx,
+    put_co,
     get_gx,
+    get_co,
+    ps,
+    owner,
     load_sem,
     send_sem,
     recv_sem,
@@ -156,6 +161,7 @@
     sibling = (i, j, 1 - g)
     across = (1 - i, j, g)
     beside = [[(i, j + 2 * s - 1, g), (i, j + 2 * s - 1, 1 - g)] for s in range(2)]
+    corner = [(1 - i, j + 2 * s - 1, g) for s in range(2)]
     exists = (j > 0, j < n_gy - 1)
 
     toward = (pl.ds(0, WIDTH), pl.ds(FACE, WIDTH))
@@ -165,9 +171,10 @@
         for n, p in enumerate(parts)
     ]
     load_data = pltpu.make_async_copy(data_hbm.at[:, 0], data, load_sem.at[3])
-    for item in load_est:
+    load_owner = pltpu.make_async_copy(owner_hbm, owner, load_sem.at[4])
+    load_ps = pltpu.make_async_copy(ps_hbm, ps, load_sem.at[5])
+    for item in [*load_est, load_owner, load_ps, load_data]:
         item.start()
-    load_data.start()
 
     def copy(number, src, dst, target):
         return pltpu.make_async_remote_copy(
@@ -191,16 +198,14 @@
         pl.semaphore_signal(barrier, inc=1, device_id=target, device_id_type=MESH)
 
     def greet(side):
-        for core in range(2):
-            pl.semaphore_signal(
-                barrier, inc=1, device_id=beside[side][core], device_id_type=MESH
-            )
+        for target in (*beside[side], corner[side]):
+            pl.semaphore_signal(barrier, inc=1, device_id=target, device_id_type=MESH)
 
     both_sides(greet)
     for item, lanes in zip(load_est[:2], toward):
         item.wait()
         own[:, lanes] = est[:, lanes].astype(BF16)
-    waits = 2 + 2 * exists[0].astype(I32) + 2 * exists[1].astype(I32)
+    waits = 2 + 3 * exists[0].astype(I32) + 3 * exists[1].astype(I32)
     pl.semaphore_wait(barrier, waits)
 
     inside = ((pl.ds(0, 16), pl.ds(0, WIDTH)), (pl.ds(32, 16), pl.ds(256, WIDTH)))
@@ -222,13 +227,8 @@
         ]
         for k in range(4)
     ]
-    pass_co = [
-        [
-            copy(7 + 2 * s + c, gx_in.at[0, *inside[s]], co_in.at[1 - s, c], beside[s][c])
-            for c in range(2)
-        ]
-        for s in range(2)
-    ]
+    send_co = [copy(7 + s, slab.at[*inside[s]], co_in.at[1 - s, 0], corner[s]) for s in range(2)]
+    pass_co = [copy(9 + s, co_in.at[s, 0], co_in.at[s, 1], sibling) for s in range(2)]
 
     def arrived(number, dst):
         copy(number, dst, dst, sibling).wait_recv()
@@ -256,7 +256,9 @@
         def _(side=side):
             gy_in[side] = jnp.zeros(gy_in.shape[1:], BF16)
             co_in[side] = jnp.zeros(co_in.shape[1:], BF16)
-            take_co[side] = jnp.zeros(take_co.shape[1:], BF16)
+
+    load_owner.wait()
+    load_ps.wait()
 
     def column(row, col):
         col = jnp.minimum(jnp.maximum(col, 0), n_gy - 1)
@@ -287,6 +289,7 @@
 
     build_forward(ps, wb, wc)
     send_gx.start()
+    both_sides(lambda s: send_co[s].start())
     build_rest(ps, i, wbt, wct, wa, wat_own, wat_far)
 
     def place(first_row, count, pair, mid, mix):
@@ -373,21 +376,18 @@
     arrived(1, gx_in.at[0])
     pass_gx.start()
 
-    def pass_ends(side):
-        for core in range(2):
-            pass_co[side][core].start()
-
-    both_sides(pass_ends)
+    for side in range(2):
+
+        @pl.when(exists[side])
+        def _(side=side):
+            arrived(7 + 1 - side, co_in.at[side, 0])
+            pass_co[side].start()
+
     select_rows(3)
     forward_chunk(3)
 
     pass_gx.wait_recv()
-    for side in range(2):
-
-        @pl.when(exists[side])
-        def _(side=side):
-            for core in range(2):
-                arrived(7 + 2 * (1 - side) + core, co_in.at[side, core])
+    both_sides(lambda s: pass_co[s].wait_recv())
 
     def lengthen(rows):
         return jnp.concatenate([rows, jnp.zeros((16 - HALO, rows.shape[1]), F32)], axis=0)
@@ -471,51 +471,28 @@
     share_gx.start()
 
     for side in range(2):
-        down = 1 - side
         for pair in range(6):
             lanes = slice(pair * LANES, (pair + 1) * LANES)
             mid, mix = fetch(64, 16, first_pair[side] + pair)
-            for core in range(2):
-                factor = f_co[side][core]
-                rows = (mid * factor[0] + mix * factor[1])[:HALO]
-                parts = [jnp.zeros((down, LANES), F32)] if down else []
-                parts += [rows, jnp.zeros((16 - HALO - down, LANES), F32)]
-                give_co[side, core, :, lanes] = jnp.concatenate(parts, axis=0).astype(BF16)
-
-    send_co = [
-        [
-            copy(12 + 2 * s + c, give_co.at[s, c], take_co.at[1 - s, c], beside[s][c])
-            for c in range(2)
-        ]
-        for s in range(2)
-    ]
-
-    def send_ends(side):
-        for core in range(2):
-            send_co[side][core].start()
-
-    both_sides(send_ends)
+            one, two = f_co[side]
+            keep_co[side, :, lanes] = mid * one[0] + mix * one[1]
+            give_co[side, :, lanes] = (mid * two[0] + mix * two[1]).astype(BF16)
+    share_co = copy(12, give_co, take_co, sibling)
+    share_co.start()
     final_gx = copy(16, put_gx, get_gx, across)
+    final_co = [copy(13 + s, put_co.at[s], get_co.at[1 - s], corner[s]) for s in range(2)]
 
     def finish_gx():
         share_gx.wait_recv()
-        keep_gx[...] = keep_gx[...] + take_gx[...].astype(F32)
-        for side in range(2):
-
-            @pl.when(exists[side])
-            def _(side=side):
-                for core in range(2):
-                    arrived(12 + 2 * (1 - side) + core, take_co.at[side, core])
-
-        for side in range(2):
-            ends = take_co[side, 0].astype(F32) + take_co[side, 1].astype(F32)
-            keep_gx[inside[side]] = keep_gx[inside[side]] + ends
-        put_gx[...] = keep_gx[...].astype(BF16)
+        put_gx[...] = (keep_gx[...] + take_gx[...].astype(F32)).astype(BF16)
         final_gx.start()
-
-    pl.loop(0, VIEWS - 1)(turn_own)
+        share_co.wait_recv()
+        put_co[...] = (keep_co[...] + take_co[...].astype(F32)).astype(BF16)
+        both_sides(lambda s: final_co[s].start())
+
+    turn_own(0)
     finish_gx()
-    turn_own(VIEWS - 1)
+    pl.loop(1, VIEWS)(turn_own)
 
     scale = live / VIEWS
     send_sides = [
@@ -570,15 +547,23 @@
             finish_own(k - 1)
     finish_own(3)
 
-    final_gx.wait_recv()
-    for q in range(4):
-        rows = get_gx[...].astype(F32)[HALO * q : HALO * q + HALO]
-        gap = jnp.zeros((16 - HALO, QUARTER), F32)
-        lanes = pl.ds(q * QUARTER, QUARTER)
+    def add_rows(rows, lanes):
+        gap = jnp.zeros((16 - HALO, rows.shape[1]), F32)
         low_rows = jnp.concatenate([rows, gap], axis=0) * (row * scale)
         high_rows = jnp.concatenate([gap, rows], axis=0) * ((1.0 - row) * scale)
         out[0, 0:16, lanes] = out[0, 0:16, lanes] + low_rows * est[0:16, lanes]
         out[0, 48:64, lanes] = out[0, 48:64, lanes] + high_rows * est[48:64, lanes]
+
+    final_gx.wait_recv()
+    for q in range(4):
+        add_rows(get_gx[...].astype(F32)[HALO * q : HALO * q + HALO], pl.ds(q * QUARTER, QUARTER))
+    for side in range(2):
+
+        @pl.when(exists[side])
+        def _(side=side):
+            arrived(13 + 1 - side, get_co.at[side])
+            add_rows(get_co[side].astype(F32)[:HALO], toward[side])
+
     for k in range(4):
         for side in range(2):
 
@@ -592,11 +577,11 @@
                     est[rows, toward[side]] * scale
                 )
 
-    for item in [send_sib, send_gx, pass_gx, share_gx, final_gx] + share_own:
+    for item in [send_sib, send_gx, pass_gx, share_gx, share_co, final_gx] + share_own:
         item.wait_send()
 
     def drain(side):
-        items = [*pass_co[side], *send_co[side]]
+        items = [send_co[side], pass_co[side], final_co[side]]
         for k in range(4):
             items += [send_gy[k][side], pass_gy[k][side], *send_sides[k][side]]
         for item in items:
@@ -609,7 +594,7 @@
     n_gy = mesh.shape["gy"]
 
     def body(estimate, views_data, point_spread, block_owner):
-        slab, ends = (48, QUARTER), (2, 2, 16, WIDTH)
+        slab, ends = (48, QUARTER), (2, 16, WIDTH)
         sides = (4, 2, 2, 16, WIDTH)
         scratch = [
             ((64, 4096), F32),
@@ -619,7 +604,7 @@
             (slab, BF16),
             ((2, *slab), BF16),
             ((2, 2, 64, WIDTH), BF16),
-            (ends, BF16),
+            ((2, *ends), BF16),
             ((SPAN_A * STEP_F, LANES), F32),
             ((SPAN_A * STEP_F, LANES), F32),
             ((512, CHUNK * LANES), BF16),
@@ -634,6 +619,7 @@
             ((VIEWS, RANK * 16, 64), BF16),
             (slab, F32),
             (slab, F32),
+            (ends, F32),
             ((64, 4096), BF16),
             (slab, BF16),
             (sides, BF16),
@@ -643,18 +629,21 @@
             (sides, BF16),
             (ends, BF16),
             (slab, BF16),
+            (ends, BF16),
             (slab, BF16),
+            (ends, BF16),
         ]
         far_spec = pl.BlockSpec(memory_space=pltpu.HBM)
-        smem = pl.BlockSpec(memory_space=pltpu.SMEM)
         return pl.pallas_call(
             functools.partial(kernel, n_gy),
             out_shape=jax.ShapeDtypeStruct((1, 64, 4096), F32),
-            in_specs=[far_spec, far_spec, smem, smem],
+            in_specs=[far_spec] * 4,
             out_specs=pl.BlockSpec(memory_space=pltpu.VMEM),
             scratch_shapes=[pltpu.VMEM(shape, kind) for shape, kind in scratch]
             + [
-                pltpu.SemaphoreType.DMA((4,)),
+                pltpu.SMEM((VIEWS, 3, RANK, TAPS), F32),
+                pltpu.SMEM((2, PILLAR, n_gy), I32),
+                pltpu.SemaphoreType.DMA((6,)),
                 pltpu.SemaphoreType.DMA((53,)),
                 pltpu.SemaphoreType.DMA((53,)),
             ],

time: 52.2 us -> 48.1 us (0.921)
  Pallas kernels: 49.7 us -> 45.5 us
    pallas_call x1, Pallas kernels: 49.7 us -> 45.5 us  [body(): pl.pallas_call(functools.partial(kernel, n_gy), out_shape=jax.ShapeDtypeS...]
where the time goes in v6:
time: 48.1 us; the launch traced here: 47.9 us
  Pallas kernels  45.5 us (95%)
  local copies, waits for them, and re-layouts  2.37 us (5%)
    pallas_call x1, Pallas kernels, body(): pl.pallas_call(functools.partial(kernel, n_gy), out_shape=jax.ShapeDtypeS...  45.5 us
    unnamed x5, local copies, waits for them, and re-layouts  2.37 us

profile of v6, /device:TPU:33, one launch (start us, length us, event | category | flops | bytes accessed | tf_op | source)
XLA Modules:
  0.0 47.9 jit_solution(34807986457234585)
XLA Ops:
  0.0 0.0 copy-start
  0.0 0.7 %copy-done = f32[4,2,3,23]{3,1,2,0:T(2,128)S(1)} copy-done((f32[4,2,3,23]{3,1,2,0:T(2,128)S(1)}, f32[4,2,3,23]{3,1,2,0:T(2,128)}, u32[]{:S(2)}) %copy-start) | copy-done | bytes 2232
  0.7 0.0 copy-start.1
  0.7 0.7 %copy-done.1 = s32[2,64,4]{1,2,0:T(4,128)S(1)} copy-done((s32[2,64,4]{1,2,0:T(4,128)S(1)}, s32[2,64,4]{1,2,0:T(4,128)}, u32[]{:S(2)}) %copy-start.1) | copy-done | bytes 2072
  1.4 45.5 %shard_map.46 = f32[1,64,4096]{2,1,0:T(8,128)S(1)} custom-call(f32[1,64,4096]{2,1,0:T(8,128)} %est_hbm.1, bf16[4,1,64,4096]{3,2,1,0:T(8,128)(2,1)} %data_hbm.1, f32[4,3,2,23]{3,2,1,0:T(2,128)S(1)} %bitcast.2, s32[2,4,64]{2,1,0:T(4,128)S(1)} %bitcast.3), custom_call_target="tpu_custom_call" | custom-call | tf_op jit(solution)/shard_map/pallas_call | solution.py:637
  46.9 1.0 %copy.6 = f32[1,64,4096]{2,1,0:T(8,128)} copy(f32[1,64,4096]{2,1,0:T(8,128)S(1)} %shard_map.46) | data formatting | bytes 2097152
Async XLA Ops:
  0.0 0.7 %copy-start = (f32[4,2,3,23]{3,1,2,0:T(2,128)S(1)}, f32[4,2,3,23]{3,1,2,0:T(2,128)}, u32[]{:S(2)}) copy-start(f32[4,2,3,23]{3,1,2,0:T(2,128)} %param.6) | copy-start | bytes 6628
  0.7 0.7 %copy-start.1 = (s32[2,64,4]{1,2,0:T(4,128)S(1)}, s32[2,64,4]{1,2,0:T(4,128)}, u32[]{:S(2)}) copy-start(s32[2,64,4]{1,2,0:T(4,128)} %param.7) | copy-start | bytes 6148

commit v7 on v6

--- a/solution.py
+++ b/solution.py
@@ -70,7 +70,7 @@
         wc[number, 128:256, :] = jnp.where(lane >= 64, base, 0.0).astype(BF16)
 
 
-def build_rest(ps, mesh_row, wbt, wct, wa, wat_own, wat_far):
+def build_rest(ps, mesh_row, wbt, wown, wside, wct, wa, wat_own, wat_far):
     tap = tap_of(ps)
     d_ct = ext_c(iota((64, LANES), 1)) - iota((64, LANES), 0) + HALO
     wct[...] = jnp.zeros_like(wct)
@@ -88,6 +88,25 @@
         low_tap, high_tap = tap(2 * pair, 1), tap(2 * pair + 1, 1)
         wbt[:, pair * LANES : (pair + 1) * LANES] = band(
             d_bt, lambda t: jnp.where(high, high_tap(t), low_tap(t))
+        ).astype(BF16)
+
+    wown[0:32, :] = wbt[0:32, :]
+    wown[32:64, :] = wbt[PAIRS : PAIRS + 32, :]
+
+    line, col = iota((32, LANES), 0), iota((32, LANES), 1)
+    line = jnp.where(line >= 16, line + PAIRS + 16, line + 32)
+    odd, entry = (col & 31) >> 4, col & 15
+    d_side = ext_b(line) - (2 * jnp.where(entry >= 8, entry + 16, entry) + odd) + HALO
+    group = col >> 5
+    for half in range(2):
+        taps = [tap(4 * half + n, 1) for n in range(4)]
+        wside[:, half * LANES : (half + 1) * LANES] = band(
+            d_side,
+            lambda t: jnp.where(
+                group < 2,
+                jnp.where(group == 0, taps[0](t), taps[1](t)),
+                jnp.where(group == 2, taps[2](t), taps[3](t)),
+            ),
         ).astype(BF16)
 
     def ext_a(place):
@@ -131,6 +150,8 @@
     v2,
     wb,
     wbt,
+    wown,
+    wside,
     wc,
     wct,
     wa,
@@ -290,7 +311,7 @@
     build_forward(ps, wb, wc)
     send_gx.start()
     both_sides(lambda s: send_co[s].start())
-    build_rest(ps, i, wbt, wct, wa, wat_own, wat_far)
+    build_rest(ps, i, wbt, wown, wside, wct, wa, wat_own, wat_far)
 
     def place(first_row, count, pair, mid, mix):
         mid_f[pl.ds(first_row * STEP_F + pair, count, stride=STEP_F), :] = mid
@@ -410,16 +431,18 @@
     forward_chunk(64 // CHUNK)
     load_data.wait()
 
-    def adjoint_front(view, back, count, first):
+    def adjoint_front(view, back, count, first, tiles):
         for term in range(RANK):
             rows = back[term * count : (term + 1) * count]
-            block = jnp.concatenate([rows[:, k * LANES : (k + 1) * LANES] for k in range(32)], axis=0)
+            block = jnp.concatenate(
+                [rows[:, n * LANES : (n + 1) * LANES] for n in range(len(tiles))], axis=0
+            )
             wide = jnp.dot(block, wct[view * RANK + term], preferred_element_type=F32)
-            for k in range(32):
+            for n, k in enumerate(tiles):
                 for odd in range(2):
                     at = first * STEP_V + (view * RANK + term) * 64 + odd * 32 + k
                     v2[pl.ds(at, count, stride=STEP_V), :] = wide[
-                        k * count : (k + 1) * count, odd * LANES : (odd + 1) * LANES
+                        n * count : (n + 1) * count, odd * LANES : (odd + 1) * LANES
                     ]
 
     def turn_far(view):
@@ -431,32 +454,44 @@
         ratio = (data[view].astype(F32) / jnp.maximum(blurred, FLOOR) * live).astype(BF16)
         data[view] = ratio
         back = jnp.dot(wat_far[view], ratio, preferred_element_type=F32).astype(BF16)
-        adjoint_front(view, back, 16, 64)
-
-    def turn_own(view):
-        back = jnp.dot(wat_own[view], data[view], preferred_element_type=F32).astype(BF16)
-        adjoint_front(view, back, 64, 0)
+        adjoint_front(view, back, 16, 64, range(32))
+
+    def turn_near(view):
+        ratio = jnp.concatenate([data[view, :, 0:1024], data[view, :, 3072:4096]], axis=1)
+        back = jnp.dot(wat_own[view], ratio, preferred_element_type=F32).astype(BF16)
+        adjoint_front(view, back, 64, 0, [*range(8), *range(24, 32)])
+
+    def turn_inner(view):
+        back = jnp.dot(wat_own[view], data[view, :, 1024:3072], preferred_element_type=F32)
+        adjoint_front(view, back.astype(BF16), 64, 0, range(8, 24))
 
     pl.loop(0, VIEWS)(turn_far)
 
-    def adjoint_rows(step):
-        start = pl.multiple_of(step * DUO * STEP_V, 8)
-        fields = jnp.concatenate(
-            [v2[pl.ds(start + k * STEP_V, 512), :].astype(BF16) for k in range(DUO)], axis=1
+    def last_pass(step, weights, pieces, count, first):
+        start = step * DUO * STEP_V
+        columns = []
+        for k in range(DUO):
+            rows = [v2[pl.ds(start + k * STEP_V + at, size), :] for at, size in pieces]
+            columns.append(jnp.concatenate(rows, axis=0).astype(BF16))
+        spread = jnp.dot(
+            weights[...], jnp.concatenate(columns, axis=1), preferred_element_type=F32
         )
-        spread = jnp.dot(wbt[...], fields, preferred_element_type=F32)
         for k in range(DUO):
-            even = spread[0:PAIRS, k * LANES : (k + 1) * LANES]
-            odd = spread[PAIRS : 2 * PAIRS, k * LANES : (k + 1) * LANES]
-            at = pl.multiple_of((step * DUO + k) * STEP_F, 8)
-            mid_f[pl.ds(at, PAIRS), :] = jnp.where(low, even, pltpu.roll(odd, 64, 1))
-            mix_f[pl.ds(at, PAIRS), :] = jnp.where(low, pltpu.roll(even, 64, 1), odd)
+            even = spread[0:count, k * LANES : (k + 1) * LANES]
+            odd = spread[count : 2 * count, k * LANES : (k + 1) * LANES]
+            near = iota((count, LANES), 1) < 64
+            at = (step * DUO + k) * STEP_F + first
+            mid_f[pl.ds(at, count), :] = jnp.where(near, even, pltpu.roll(odd, 64, 1))
+            mix_f[pl.ds(at, count), :] = jnp.where(near, pltpu.roll(even, 64, 1), odd)
+
+    whole = [(0, 512)]
+    sides_only = [(at + edge, 8) for at in range(0, 512, 32) for edge in (0, 24)]
 
     def fetch(first_row, count, pair):
         at = pl.ds(first_row * STEP_F + pair, count, stride=STEP_F)
         return mid_f[at, :], mix_f[at, :]
 
-    adjoint_rows(64 // DUO)
+    last_pass(64 // DUO, wbt, whole, PAIRS, 0)
     for q in range(4):
         for number in range(8):
             lanes = slice(number * LANES, (number + 1) * LANES)
@@ -490,9 +525,9 @@
         put_co[...] = (keep_co[...] + take_co[...].astype(F32)).astype(BF16)
         both_sides(lambda s: final_co[s].start())
 
-    turn_own(0)
+    pl.loop(0, 2)(turn_near)
     finish_gx()
-    pl.loop(1, VIEWS)(turn_own)
+    pl.loop(2, VIEWS)(turn_near)
 
     scale = live / VIEWS
     send_sides = [
@@ -511,7 +546,7 @@
     ]
 
     def own_rows(k):
-        adjoint_rows(k)
+        last_pass(k, wside, sides_only, 16, 32)
         for side in range(2):
             for pair in range(6):
                 lanes = pl.ds(pair * LANES, LANES)
@@ -527,6 +562,7 @@
         both_sides(send)
 
     def own_block(k):
+        last_pass(k, wown, whole, 32, 0)
         for pair in range(32):
             lanes = pl.ds(pair * LANES, LANES)
             mid, mix = fetch(16 * k, 16, pair)
@@ -541,6 +577,7 @@
 
     for k in range(4):
         own_rows(k)
+    pl.loop(0, VIEWS)(turn_inner)
     for k in range(4):
         own_block(k)
         if k:
@@ -612,6 +649,8 @@
             ((SPAN_A * STEP_V, LANES), F32),
             ((512, 96), BF16),
             ((96, 512), BF16),
+            ((64, 512), BF16),
+            ((32, 256), BF16),
             ((8, 256, 128), BF16),
             ((8, 128, 256), BF16),
             ((VIEWS, 64, 2 * SPAN_A), BF16),
@@ -653,8 +692,8 @@
         )(
             estimate,
             views_data,
-            point_spread.transpose(0, 2, 1, 3),
-            block_owner.transpose(0, 2, 1),
+            pltpu.with_memory_space_constraint(point_spread.transpose(0, 2, 1, 3), pltpu.HBM),
+            pltpu.with_memory_space_constraint(block_owner.transpose(0, 2, 1), pltpu.HBM),
         )
 
     placed = (P(("gx", "gy", "gz"), None, None), P(None, ("gx", "gy", "gz"), None, None), P(), P())

time: 48.1 us -> 45.5 us (0.946)
  local copies, waits for them, and re-layouts: 2.37 us -> 0.97 us
  Pallas kernels: 45.5 us -> 44.5 us
    unnamed x5 -> x1, local copies, waits for them, and re-layouts: 2.37 us -> 0.97 us
    pallas_call x1, Pallas kernels: 45.5 us -> 44.5 us  [body(): pl.pallas_call(functools.partial(kernel, n_gy), out_shape=jax.ShapeDtypeS...]
where the time goes in v7:
time: 45.5 us; the launch traced here: 45.4 us
  Pallas kernels  44.5 us (98%)
  local copies, waits for them, and re-layouts  0.97 us (2%)
    pallas_call x1, Pallas kernels, body(): pl.pallas_call(functools.partial(kernel, n_gy), out_shape=jax.ShapeDtypeS...  44.5 us
    unnamed x1, local copies, waits for them, and re-layouts  0.97 us

profile of v7, /device:TPU:33, one launch (start us, length us, event | category | flops | bytes accessed | tf_op | source)
XLA Modules:
  0.0 45.4 jit_solution(780092096407189688)
XLA Ops:
  0.0 44.5 %shard_map.46 = f32[1,64,4096]{2,1,0:T(8,128)S(1)} custom-call(f32[1,64,4096]{2,1,0:T(8,128)} %est_hbm.1, bf16[4,1,64,4096]{3,2,1,0:T(8,128)(2,1)} %data_hbm.1, f32[4,3,2,23]{3,2,1,0:T(2,128)} %bitcast.2, s32[2,4,64]{2,1,0:T(4,128)} %bitcast.3), custom_call_target="tpu_custom_call" | custom-call | tf_op jit(solution)/shard_map/pallas_call | solution.py:676
  44.5 1.0 %copy.6 = f32[1,64,4096]{2,1,0:T(8,128)} copy(f32[1,64,4096]{2,1,0:T(8,128)S(1)} %shard_map.46) | data formatting | bytes 2097152

commit v8 on v7

--- a/solution.py
+++ b/solution.py
@@ -55,32 +55,23 @@
     return tap
 
 
-def build_forward(ps, wb, wc):
+def build_forward(ps, wb, wct):
     tap = tap_of(ps)
     d_b = ext_b(iota((64, 96), 1)) - parity_b(iota((64, 96), 0)) + HALO
-    lane = iota((LANES, LANES), 1)
-    d_c = ext_c(iota((LANES, LANES), 0)) - jnp.where(lane >= 64, lane - 64, lane) + HALO
+    d_ct = ext_c(iota((64, LANES), 1)) - iota((64, LANES), 0) + HALO
+    wct[...] = jnp.zeros_like(wct)
 
     @pl.loop(0, VIEWS * RANK)
     def _(number):
         start = pl.multiple_of(number * 64, 64)
         wb[pl.ds(start, 64), :] = band(d_b, tap(number, 1)).astype(BF16)
-        base = band(d_c, tap(number, 2))
-        wc[number, 0:128, :] = jnp.where(lane < 64, base, 0.0).astype(BF16)
-        wc[number, 128:256, :] = jnp.where(lane >= 64, base, 0.0).astype(BF16)
-
-
-def build_rest(ps, mesh_row, wbt, wown, wside, wct, wa, wat_own, wat_far):
-    tap = tap_of(ps)
-    d_ct = ext_c(iota((64, LANES), 1)) - iota((64, LANES), 0) + HALO
-    wct[...] = jnp.zeros_like(wct)
-
-    @pl.loop(0, VIEWS * RANK)
-    def _(number):
         base = band(d_ct, tap(number, 2)).astype(BF16)
         wct[number, 0:64, 0:128] = base
         wct[number, 64:128, 128:256] = base
 
+
+def build_rest(ps, mesh_row, wbt, wown, wside, wa, wat_own, wat_far):
+    tap = tap_of(ps)
     col = iota((96, LANES), 1)
     high = col >= 64
     d_bt = ext_b(iota((96, LANES), 0)) - parity_b(jnp.where(high, col - 64, col)) + HALO
@@ -152,7 +143,6 @@
     wbt,
     wown,
     wside,
-    wc,
     wct,
     wa,
     wat_own,
@@ -308,10 +298,10 @@
     f_co = [[factors(e, exists[s]) for e in column(1 - i, j + 2 * s - 1)] for s in range(2)]
     live = valid.astype(F32)
 
-    build_forward(ps, wb, wc)
+    build_forward(ps, wb, wct)
     send_gx.start()
     both_sides(lambda s: send_co[s].start())
-    build_rest(ps, i, wbt, wown, wside, wct, wa, wat_own, wat_far)
+    build_rest(ps, i, wbt, wown, wside, wa, wat_own, wat_far)
 
     def place(first_row, count, pair, mid, mix):
         mid_f[pl.ds(first_row * STEP_F + pair, count, stride=STEP_F), :] = mid
@@ -326,6 +316,11 @@
             first * factor[0][0] + second * factor[1][0],
             first * factor[0][1] + second * factor[1][1],
         )
+
+    for term in range(RANK):
+        for unused in range(76, SPAN_A):
+            start = term * SPAN_A + unused
+            t2[pl.ds(start, VIEWS * 32, stride=STEP_T), :] = jnp.zeros((VIEWS * 32, LANES), F32)
 
     for pair in range(44, PAIRS):
         place(0, SPAN_A, pair, jnp.zeros((SPAN_A, LANES), F32), jnp.zeros((SPAN_A, LANES), F32))
@@ -356,8 +351,8 @@
 
     low = iota((PAIRS, LANES), 1) < 64
 
-    def forward_chunk(chunk):
-        for two in range(CHUNK // 2):
+    def forward_chunk(chunk, count=CHUNK):
+        for two in range(count // 2):
             parts = []
             for one in range(2):
                 start = pl.multiple_of((chunk * CHUNK + two * 2 + one) * STEP_F, 8)
@@ -379,12 +374,14 @@
                         ],
                         axis=1,
                     )
-                    for a in range(CHUNK)
+                    for a in range(count)
                 ],
                 axis=0,
             )
-            second = jnp.dot(block, wc[number], preferred_element_type=F32)
-            for a in range(CHUNK):
+            second = lax.dot_general(
+                block, wct[number], (((1,), (1,)), ((), ())), preferred_element_type=F32
+            )
+            for a in range(count):
                 start = view * 32 * STEP_T + term * SPAN_A + chunk * CHUNK + a
                 t2[pl.ds(start, 32, stride=STEP_T), :] = second[a * 32 : a * 32 + 32, :]
 
@@ -428,7 +425,7 @@
             mid, mix = blend([lengthen(r) for r in rows], f_co[side])
             place(64, 16, first_pair[side] + pair, mid, mix)
 
-    forward_chunk(64 // CHUNK)
+    forward_chunk(64 // CHUNK, 12)
     load_data.wait()
 
     def adjoint_front(view, back, count, first, tiles):
@@ -451,7 +448,7 @@
             [t2[pl.ds(start + k * STEP_T, 2 * SPAN_A), :].astype(BF16) for k in range(32)], axis=1
         )
         blurred = jnp.dot(wa[view], fields, preferred_element_type=F32)
-        ratio = (data[view].astype(F32) / jnp.maximum(blurred, FLOOR) * live).astype(BF16)
+        ratio = (data[view].astype(F32) / jnp.maximum(blurred, FLOOR)).astype(BF16)
         data[view] = ratio
         back = jnp.dot(wat_far[view], ratio, preferred_element_type=F32).astype(BF16)
         adjoint_front(view, back, 16, 64, range(32))
@@ -467,16 +464,16 @@
 
     pl.loop(0, VIEWS)(turn_far)
 
-    def last_pass(step, weights, pieces, count, first):
+    def last_pass(step, weights, pieces, count, first, rows_done=DUO):
         start = step * DUO * STEP_V
         columns = []
-        for k in range(DUO):
+        for k in range(rows_done):
             rows = [v2[pl.ds(start + k * STEP_V + at, size), :] for at, size in pieces]
             columns.append(jnp.concatenate(rows, axis=0).astype(BF16))
         spread = jnp.dot(
             weights[...], jnp.concatenate(columns, axis=1), preferred_element_type=F32
         )
-        for k in range(DUO):
+        for k in range(rows_done):
             even = spread[0:count, k * LANES : (k + 1) * LANES]
             odd = spread[count : 2 * count, k * LANES : (k + 1) * LANES]
             near = iota((count, LANES), 1) < 64
@@ -491,7 +488,7 @@
         at = pl.ds(first_row * STEP_F + pair, count, stride=STEP_F)
         return mid_f[at, :], mix_f[at, :]
 
-    last_pass(64 // DUO, wbt, whole, PAIRS, 0)
+    last_pass(64 // DUO, wbt, whole, PAIRS, 0, 12)
     for q in range(4):
         for number in range(8):
             lanes = slice(number * LANES, (number + 1) * LANES)
@@ -566,14 +563,14 @@
         for pair in range(32):
             lanes = pl.ds(pair * LANES, LANES)
             mid, mix = fetch(16 * k, 16, pair)
-            out[0, 16 * k : 16 * k + 16, lanes] = mid
+            out[0, 16 * k : 16 * k + 16, lanes] = mid * (est[16 * k : 16 * k + 16, lanes] * scale)
             give_own[16 * k : 16 * k + 16, lanes] = (mix * f_sib[1]).astype(BF16)
         share_own[k].start()
 
     def finish_own(k):
         share_own[k].wait_recv()
         rows = slice(16 * k, 16 * k + 16)
-        out[0, rows] = (out[0, rows] + take_own[rows].astype(F32)) * (est[rows] * scale)
+        out[0, rows] = out[0, rows] + take_own[rows].astype(F32) * (est[rows] * scale)
 
     for k in range(4):
         own_rows(k)
@@ -582,7 +579,6 @@
         own_block(k)
         if k:
             finish_own(k - 1)
-    finish_own(3)
 
     def add_rows(rows, lanes):
         gap = jnp.zeros((16 - HALO, rows.shape[1]), F32)
@@ -613,6 +609,8 @@
                 out[0, rows, toward[side]] = out[0, rows, toward[side]] + total * (
                     est[rows, toward[side]] * scale
                 )
+
+    finish_own(3)
 
     for item in [send_sib, send_gx, pass_gx, share_gx, share_co, final_gx] + share_own:
         item.wait_send()
@@ -651,7 +649,6 @@
             ((96, 512), BF16),
             ((64, 512), BF16),
             ((32, 256), BF16),
-            ((8, 256, 128), BF16),
             ((8, 128, 256), BF16),
             ((VIEWS, 64, 2 * SPAN_A), BF16),
             ((VIEWS, RANK * 64, 64), BF16),

time: 45.5 us -> 45 us (0.989)
  Pallas kernels: 44.5 us -> 43.9 us
    pallas_call x1, Pallas kernels: 44.5 us -> 43.9 us  [body(): pl.pallas_call(functools.partial(kernel, n_gy), out_shape=jax.ShapeDtypeS...]
where the time goes in v8:
time: 45 us; the launch traced here: 44.9 us
  Pallas kernels  43.9 us (98%)
  local copies, waits for them, and re-layouts  0.97 us (2%)
    pallas_call x1, Pallas kernels, body(): pl.pallas_call(functools.partial(kernel, n_gy), out_shape=jax.ShapeDtypeS...  43.9 us
    unnamed x1, local copies, waits for them, and re-layouts  0.97 us

profile of v8, /device:TPU:33, one launch (start us, length us, event | category | flops | bytes accessed | tf_op | source)
XLA Modules:
  0.0 44.9 jit_solution(13210894685277001618)
XLA Ops:
  0.0 43.9 %shard_map.46 = f32[1,64,4096]{2,1,0:T(8,128)S(1)} custom-call(f32[1,64,4096]{2,1,0:T(8,128)} %est_hbm.1, bf16[4,1,64,4096]{3,2,1,0:T(8,128)(2,1)} %data_hbm.1, f32[4,3,2,23]{3,2,1,0:T(2,128)} %bitcast.2, s32[2,4,64]{2,1,0:T(4,128)} %bitcast.3), custom_call_target="tpu_custom_call" | custom-call | tf_op jit(solution)/shard_map/pallas_call | solution.py:673
  43.9 1.0 %copy.6 = f32[1,64,4096]{2,1,0:T(8,128)} copy(f32[1,64,4096]{2,1,0:T(8,128)S(1)} %shard_map.46) | data formatting | bytes 2097152

commit v9 on v8

--- a/solution.py
+++ b/solution.py
@@ -299,9 +299,9 @@
     live = valid.astype(F32)
 
     build_forward(ps, wb, wct)
+    build_rest(ps, i, wbt, wown, wside, wa, wat_own, wat_far)
     send_gx.start()
     both_sides(lambda s: send_co[s].start())
-    build_rest(ps, i, wbt, wown, wside, wa, wat_own, wat_far)
 
     def place(first_row, count, pair, mid, mix):
         mid_f[pl.ds(first_row * STEP_F + pair, count, stride=STEP_F), :] = mid

time: 45 us -> 45 us (level)
  no operation moved by 1% of the time
where the time goes in v9:
time: 45 us; the launch traced here: 44.9 us
  Pallas kernels  43.9 us (98%)
  local copies, waits for them, and re-layouts  0.97 us (2%)
    pallas_call x1, Pallas kernels, body(): pl.pallas_call(functools.partial(kernel, n_gy), out_shape=jax.ShapeDtypeS...  43.9 us
    unnamed x1, local copies, waits for them, and re-layouts  0.97 us

profile of v9, /device:TPU:33, one launch (start us, length us, event | category | flops | bytes accessed | tf_op | source)
XLA Modules:
  0.0 44.9 jit_solution(335844360827982869)
XLA Ops:
  0.0 43.9 %shard_map.46 = f32[1,64,4096]{2,1,0:T(8,128)S(1)} custom-call(f32[1,64,4096]{2,1,0:T(8,128)} %est_hbm.1, bf16[4,1,64,4096]{3,2,1,0:T(8,128)(2,1)} %data_hbm.1, f32[4,3,2,23]{3,2,1,0:T(2,128)} %bitcast.2, s32[2,4,64]{2,1,0:T(4,128)} %bitcast.3), custom_call_target="tpu_custom_call" | custom-call | tf_op jit(solution)/shard_map/pallas_call | solution.py:673
  43.9 1.0 %copy.6 = f32[1,64,4096]{2,1,0:T(8,128)} copy(f32[1,64,4096]{2,1,0:T(8,128)S(1)} %shard_map.46) | data formatting | bytes 2097152
